TPU v7x, 32 devices: a whole 2x2x4 slice. The times are simulated.
32 devices in a mesh: groups: 2 (over y), seq: 16 (over z, x, core).
Axes of the slice: x: 2, y: 2, z: 4, core: 2. Of those that a mesh axis runs over, the one named last changes fastest.
Arguments:
- inputs: bfloat16 [16384, 768], P(('groups', 'seq')), parts along dimension 0, may hold values from -400 to 400
- projection: bfloat16 [768, 2304], P('seq'), may hold values from -2 to 2
- positions: int32 [16384], P(('groups', 'seq')), parts along dimension 0, may hold values from 0 to 1024, as said below
- segments: int32 [16384], P(('groups', 'seq')), parts along dimension 0, may hold values from 0 to 7, as said below
- context_grad: bfloat16 [16384, 768], P(('groups', 'seq')), parts along dimension 0, may hold values from -6 to 6
Outputs:
- context: bfloat16 [16384, 768], P(('groups', 'seq')), parts along dimension 0
- input_grad: bfloat16 [16384, 768], P(('groups', 'seq')), parts along dimension 0
- projection_grad: float32 [1536, 2304], P(('groups', 'seq')), parts along dimension 0
There are 2 independent parts, one for each index of `groups`. A program takes and returns all parts, laid end to end along the dimension named above; an argument that names none is the same for every part. Nothing has to cross between parts.
Inputs may be any that keep to these rules, and one draw needn't show every extreme that they name: `segments`: segment ids never fall along the sequence; the first token has id 0, the last id 8 - 1, and every id in between occurs. positions are 0 at the first token of every segment; within a segment a position is the segment's time index capped at 1024, and the time index rises by 0 to 3 from one token to the next.
All inputs are finite; a program needn't handle non-finite values.
Results may differ from a plain program's by a relative error of at most 0.03.
The roundings to bfloat16 on the way count: a program that leaves them out, or rounds other values in their place, can miss the bound.
Values may be sent and summed in bfloat16 or wider, within the bound.
A program may use at most 128 MiB of HBM per device.

v0:
```python
import math

import jax
import jax.numpy as jnp
from jax import lax
from jax.sharding import PartitionSpec as P

D = 768
H = 12
HD = 64
W = 1024


EPSILON = 1e-05
SCORE_SCALE = 0.125
MASKED_SCORE = -1e30


def shifted(value, axis, steps):
    count = lax.axis_size(axis)
    leading, last = (max(0, -steps), min(count, count - steps))
    return lax.ppermute(value, axis, [(source, source + steps) for source in range(leading, last)])


def rotary_tables(positions):
    half_size = HD // 2
    frequency = jnp.exp(-math.log(10000.0) * jnp.arange(half_size, dtype=jnp.float32) / half_size)
    angle = positions.astype(jnp.float32)[:, None] * frequency[None, :]
    return (jnp.cos(angle)[:, None, :], jnp.sin(angle)[:, None, :])


def rotate(tensor, cosine_table, sine_table):
    first_half = tensor[..., : HD // 2]
    second_half = tensor[..., HD // 2 :]
    return jnp.concatenate(
        [
            first_half * cosine_table - second_half * sine_table,
            second_half * cosine_table + first_half * sine_table,
        ],
        axis=-1,
    )


def unrotate(tensor, cosine_table, sine_table):
    first_half = tensor[..., : HD // 2]
    second_half = tensor[..., HD // 2 :]
    return jnp.concatenate(
        [
            first_half * cosine_table + second_half * sine_table,
            second_half * cosine_table - first_half * sine_table,
        ],
        axis=-1,
    )


def heads_first(tensor):
    return jnp.transpose(tensor.reshape(tensor.shape[0], H, HD), (1, 0, 2))


def flat_rows(tensor):
    return jnp.transpose(tensor, (1, 0, 2)).reshape(tensor.shape[1], D)


def head_block(queries, key_block, value_block, out_grads, allowed):
    scores = jnp.dot(queries, key_block.T, preferred_element_type=jnp.float32) * SCORE_SCALE
    masked = jnp.where(allowed, scores, MASKED_SCORE)
    row_max = jnp.max(masked, axis=1, keepdims=True)
    log_total = row_max + jnp.log(jnp.sum(jnp.exp(masked - row_max), axis=1, keepdims=True))
    weights = jnp.exp(masked - log_total)
    probs = weights.astype(jnp.bfloat16)
    context = jnp.dot(probs, value_block, preferred_element_type=jnp.float32).astype(jnp.bfloat16)
    row_delta = jnp.sum(out_grads.astype(jnp.float32) * context.astype(jnp.float32), axis=1)
    dprobs = jnp.dot(out_grads, value_block.T, preferred_element_type=jnp.float32)
    dscores = (weights * (dprobs - row_delta[:, None])).astype(jnp.bfloat16)
    query_grad = jnp.dot(dscores, key_block, preferred_element_type=jnp.float32) * SCORE_SCALE
    key_grad = jnp.dot(dscores.T, queries, preferred_element_type=jnp.float32) * SCORE_SCALE
    value_grad = jnp.dot(probs.T, out_grads, preferred_element_type=jnp.float32)
    return (context, query_grad, key_grad, value_grad, log_total[:, 0], row_delta)


def local(inputs, projection, positions, segments, context_grad):
    row_count = inputs.shape[0]
    device_count = lax.axis_size("seq")
    device_index = lax.axis_index("seq")
    first_global = device_index * row_count
    reach = W // row_count
    grad_scale = (row_count * device_count) ** (-0.5)
    x_float = inputs.astype(jnp.float32)
    inv_rms = lax.rsqrt(jnp.mean(x_float * x_float, axis=1, keepdims=True) + EPSILON)
    scaled = x_float * inv_rms
    normed = scaled.astype(jnp.bfloat16)
    columns = normed
    projected = jnp.dot(
        columns,
        lax.all_gather(projection, "seq", axis=0, tiled=True),
        preferred_element_type=jnp.float32,
    )
    cosine_table, sine_table = rotary_tables(positions)
    q_rot = (
        rotate(projected[:, :D].reshape(row_count, H, HD), cosine_table, sine_table)
        .astype(jnp.bfloat16)
        .reshape(row_count, D)
    )
    k_rot = (
        rotate(projected[:, D : 2 * D].reshape(row_count, H, HD), cosine_table, sine_table)
        .astype(jnp.bfloat16)
        .reshape(row_count, D)
    )
    values = projected[:, 2 * D :].astype(jnp.bfloat16)
    seg_value = segments.astype(jnp.bfloat16)
    earlier = [
        shifted((k_rot, values, seg_value), "seq", distance) for distance in range(reach, 0, -1)
    ]
    key_rows = jnp.concatenate([entry[0] for entry in earlier] + [k_rot], axis=0)
    value_rows = jnp.concatenate([entry[1] for entry in earlier] + [values], axis=0)
    key_seg = jnp.concatenate([entry[2] for entry in earlier] + [seg_value], axis=0).astype(
        jnp.float32
    )
    query_seg = seg_value.astype(jnp.float32)
    key_index = first_global - W + jnp.arange(W + row_count, dtype=jnp.int32)
    key_heads = heads_first(key_rows)
    value_heads = heads_first(value_rows)
    query_heads = heads_first(q_rot)
    grad_heads = heads_first(context_grad)
    keep_from = 0
    key_acc = jnp.zeros((H, W + row_count - keep_from, HD), jnp.float32)
    value_acc = jnp.zeros((H, W + row_count - keep_from, HD), jnp.float32)
    block_rows = min(512, row_count)
    key_span = block_rows + W
    context_parts, query_parts, total_parts, delta_parts = ([], [], [], [])
    query_index = first_global + 0 + jnp.arange(block_rows, dtype=jnp.int32)
    offsets = query_index[:, None] - key_index[None, :]
    allowed = (
        (offsets >= 0)
        & (offsets < W)
        & (key_index[None, :] >= 0)
        & (query_seg[:, None] == key_seg[None, :])
    )
    from_col = max(keep_from, 0)
    results = lax.map(
        lambda operands: head_block(operands[0], operands[1], operands[2], operands[3], allowed),
        (query_heads, key_heads, value_heads, grad_heads),
    )
    context_parts.append(results[0])
    query_parts.append(results[1])
    total_parts.append(results[4])
    delta_parts.append(results[5])
    offset = from_col - keep_from
    key_acc = key_acc.at[:, offset : offset + key_span - from_col].add(results[2])
    value_acc = value_acc.at[:, offset : offset + key_span - from_col].add(results[3])
    context = flat_rows(context_parts[0])
    query_grad = jnp.transpose(query_parts[0], (1, 0, 2))
    query_part = (
        unrotate(query_grad, cosine_table, sine_table).reshape(row_count, D).astype(jnp.bfloat16)
    )
    own_key_grad = flat_rows(key_acc[:, W:])
    own_value_grad = flat_rows(value_acc[:, W:])
    for distance in range(1, reach + 1):
        offset = (reach - distance) * row_count
        received = (
            shifted(
                flat_rows(key_acc[:, offset : offset + row_count]).astype(jnp.bfloat16),
                "seq",
                -distance,
            ).astype(jnp.float32),
            shifted(
                flat_rows(value_acc[:, offset : offset + row_count]).astype(jnp.bfloat16),
                "seq",
                -distance,
            ).astype(jnp.float32),
        )
        own_key_grad = own_key_grad + received[0]
        own_value_grad = own_value_grad + received[1]
    key_lin = unrotate(own_key_grad.reshape(row_count, H, HD), cosine_table, sine_table).reshape(
        row_count, D
    )
    kv_part = jnp.concatenate([key_lin, own_value_grad], axis=1).astype(jnp.bfloat16)
    dqkv = jnp.concatenate([query_part, kv_part], axis=1)
    normed_grad = jnp.dot(
        dqkv,
        lax.all_gather(projection, "seq", axis=0, tiled=True).T,
        preferred_element_type=jnp.float32,
    )
    input_grad = (
        inv_rms * (normed_grad - scaled * jnp.mean(normed_grad * scaled, axis=1, keepdims=True))
    ).astype(jnp.bfloat16)
    columns = normed
    projection_grad = (
        lax.psum_scatter(
            jnp.dot(columns.T, dqkv, preferred_element_type=jnp.float32),
            "seq",
            scatter_dimension=0,
            tiled=True,
        )
        * grad_scale
    )
    return (context, input_grad, projection_grad)


def solution(mesh):
    in_specs = (
        P(("groups", "seq"), None),
        P("seq", None),
        P(("groups", "seq")),
        P(("groups", "seq")),
        P(("groups", "seq"), None),
    )
    out_specs = (P(("groups", "seq"), None), P(("groups", "seq"), None), P(("groups", "seq"), None))
    return jax.shard_map(local, mesh=mesh, in_specs=in_specs, out_specs=out_specs, check_vma=False)
```

profile of v0, /device:TPU:11, one launch (start us, length us, event | category | flops | bytes accessed | tf_op | source)
XLA Modules:
  0.0 417.6 jit_solution(860616682711346561)
XLA Ops:
  8.6 3.7 collective-permute-start.3
  12.4 3.1 collective-permute-start.2
  16.2 2.3 copy.20
  19.1 39.3 %all-gather.2.cloned.1.call-done = bf16[768,2304]{1,0:T(8,128)(2,1)} async-done(((bf16[48,2304]{1,0:T(8,128)(2,1)}), bf16[768,2304]{1,0:T(8,128)(2,1)}) %all-gather.2.cloned.1.call-update) | async-done | bytes 3538960 | tf_op jit(solution)/shard_map/all_gather | solution.py:95
  58.5 4.1 fusion.52
  64.9 3.5 collective-permute-start.5
  73.7 2.4 collective-permute-start.1
  76.1 3.1 collective-permute-start
  80.1 3.2 collective-permute-done.5
  83.2 17.6 %collective-permute-done.4 = bf16[512,768]{1,0:T(8,128)(2,1)} collective-permute-done((bf16[512,768]{1,0:T(8,128)(2,1)}, bf16[512,768]{1,0:T(8,128)(2,1)}, u32[]{:S(2)}, u32[]{:S(2)}) %collective-permute-start.4) | collective-permute-done | bytes 786464 | tf_op jit(solution)/shard_map/ppermute | solution.py:22
  102.6 2.5 copy.19
  105.1 6.3 %collective-permute-done.1 = bf16[512,768]{0,1:T(8,128)(2,1)} collective-permute-done((bf16[512,768]{0,1:T(8,128)(2,1)}, bf16[512,768]{0,1:T(8,128)(2,1)}, u32[]{:S(2)}, u32[]{:S(2)}) %collective-permute-start.1) | collective-permute-done | bytes 786464 | tf_op jit(solution)/shard_map/ppermute | solution.py:22
  111.3 8.9 %collective-permute-done = bf16[512,768]{0,1:T(8,128)(2,1)} collective-permute-done((bf16[512,768]{0,1:T(8,128)(2,1)}, bf16[512,768]{0,1:T(8,128)(2,1)}, u32[]{:S(2)}, u32[]{:S(2)}) %collective-permute-start) | collective-permute-done | bytes 786464 | tf_op jit(solution)/shard_map/ppermute | solution.py:22
  122.0 140.9 %while.21 = (s32[]{:T(128)}, bf16[12,512,64]{1,2,0:T(8,128)(2,1)}, f32[12,512,64]{1,2,0:T(8,128)}, f32[12,1536,64]{1,2,0:T(8,128)}, f32[12,1536,64]{1,2,0:T(8,12...) while((s32[]{:T(128)}, bf16[12,512,64]{1,2,0:T(8,128)(2,1)}, ...), condition=%wide.region_5.6_spmd.clone, body=%wide.region_1.5_spmd.clone.sunk | while | flops 620002304 | bytes 22726808 | solution.py:140
  124.2 2.3 bitcast_dynamic-update-slice_fusion.2
  129.1 2.3 fusion.90
  136.0 2.3 bitcast_dynamic-update-slice_fusion.2
  140.9 2.3 fusion.90
  147.7 2.3 bitcast_dynamic-update-slice_fusion.2
  152.6 2.3 fusion.90
  159.5 2.3 bitcast_dynamic-update-slice_fusion.2
  164.3 2.3 fusion.90
  171.2 2.3 bitcast_dynamic-update-slice_fusion.2
  176.1 2.3 fusion.90
  182.9 2.3 bitcast_dynamic-update-slice_fusion.2
  187.8 2.3 fusion.90
  194.6 2.3 bitcast_dynamic-update-slice_fusion.2
  199.5 2.3 fusion.90
  206.3 2.3 bitcast_dynamic-update-slice_fusion.2
  211.2 2.3 fusion.90
  218.1 2.3 bitcast_dynamic-update-slice_fusion.2
  223.0 2.3 fusion.90
  229.9 2.3 bitcast_dynamic-update-slice_fusion.2
  234.8 2.3 fusion.90
  241.6 2.3 bitcast_dynamic-update-slice_fusion.2
  246.5 2.3 fusion.90
  253.4 2.3 bitcast_dynamic-update-slice_fusion.2
  258.3 2.3 fusion.90
  263.0 2.8 convert.39
  266.0 4.0 collective-permute-start.7
  276.0 2.6 collective-permute-start.8
  278.7 8.4 %collective-permute-done.7 = bf16[512,768]{0,1:T(8,128)(2,1)S(1)} collective-permute-done((bf16[512,768]{0,1:T(8,128)(2,1)S(1)}, bf16[512,768]{0,1:T(8,128)(2,1)S(1)}, u32[]{:S(2)}, u32[]{:S(2)}) %collective-permute-start.7) | collective-permute-done | bytes 786464 | tf_op jit(solution)/shard_map/ppermute | solution.py:22
  287.0 5.6 %collective-permute-done.6 = bf16[512,768]{0,1:T(8,128)(2,1)S(1)} collective-permute-done((bf16[512,768]{0,1:T(8,128)(2,1)S(1)}, bf16[512,768]{0,1:T(8,128)(2,1)S(1)}, u32[]{:S(2)}, u32[]{:S(2)}) %collective-permute-start.6) | collective-permute-done | bytes 786464 | tf_op jit(solution)/shard_map/ppermute | solution.py:22
  293.8 10.1 %collective-permute-done.9 = bf16[512,768]{0,1:T(8,128)(2,1)S(1)} collective-permute-done((bf16[512,768]{0,1:T(8,128)(2,1)S(1)}, bf16[512,768]{0,1:T(8,128)(2,1)S(1)}, u32[]{:S(2)}, u32[]{:S(2)}) %collective-permute-start.9) | collective-permute-done | bytes 786464 | tf_op jit(solution)/shard_map/ppermute | solution.py:22
  303.9 10.6 %collective-permute-done.8 = bf16[512,768]{0,1:T(8,128)(2,1)S(1)} collective-permute-done((bf16[512,768]{0,1:T(8,128)(2,1)S(1)}, bf16[512,768]{0,1:T(8,128)(2,1)S(1)}, u32[]{:S(2)}, u32[]{:S(2)}) %collective-permute-start.8) | collective-permute-done | bytes 786464 | tf_op jit(solution)/shard_map/ppermute | solution.py:22
  314.8 5.1 %fusion.49 = f32[768,2304]{1,0:T(8,128)} fusion(bf16[512,768]{0,1:T(8,128)(2,1)S(1)} %fusion.47, bf16[512,768]{0,1:T(8,128)(2,1)S(1)} %bitcast.140, bf16[512,768]{0,1:T(8,128)(2,1)S(1)} %bitcast.138, bf16[512,768]{1,0:T(8,128)(2,1)S(1)} %copy-done.2, f32[512]{0:T(512)S(1)} %add_rsqrt_fusion), kind=kOutput, calls=%fused_computation.68 | convolution fusion | flops 1820196864 | bytes 10225664 | tf_op jit(solution)/shard_map/dot_general | solution.py:190
  322.3 4.5 %fusion.41 = (f32[512]{0:T(512)S(1)}, f32[512,768]{1,0:T(8,128)S(1)}) fusion(bf16[512,768]{1,0:T(8,128)(2,1)S(1)} %copy-done.2, f32[512]{0:T(512)S(1)} %add_rsqrt_fusion, bf16[768,2304]{1,0:T(8,128)(2,1)} %all-gather.2.cloned.1.call-done, bf16[512,768]{0,1:T(8,128)(2,1)} %copy-done.7, bf16[512,768]{0,1:T(8,128)(2,1)S(1)} %bitcast.141, ...), kind=kOutput, calls=%fused_computation.56 | convolution fusion | flops 1820589568 | bytes 8261632 | tf_op jit(solution)/shard_map/dot_general | solution.py:179
  328.0 80.9 %reduce-scatter.2.cloned.1.call-done = f32[48,2304]{1,0:T(8,128)} async-done(((f32[768,2304]{1,0:T(8,128)}), f32[48,2304]{1,0:T(8,128)}) %reduce-scatter.2.cloned.1.call-update) | async-done | bytes 442384 | tf_op jit(solution)/shard_map/reduce_scatter | solution.py:189
  (146 shorter events, 113.9 us)
Async XLA Ops:
  7.2 11.4 %copy-start.1 = (bf16[512,768]{1,0:T(8,128)(2,1)S(1)}, bf16[512,768]{1,0:T(8,128)(2,1)}, u32[]{:S(2)}) copy-start(bf16[512,768]{1,0:T(8,128)(2,1)} %param.15) | copy-start | bytes 2359300
  7.2 51.3 %all-gather.2.cloned.1.call-start = ((), (), s32[]{:S(2)}) async-start(), calls=%async_computation.1 | async-start | bytes 3760128 | tf_op jit(solution)/shard_map/all_gather | solution.py:95
  7.9 401.0 %reduce-scatter.2.cloned.1.call-start = ((), (), s32[]{:S(2)}) async-start(), calls=%async_computation.2 | async-start | bytes 7520256 | tf_op jit(solution)/shard_map/reduce_scatter | solution.py:189
  8.6 67.5 %collective-permute-start.3 = (bf16[512]{0:T(512)(128)(2,1)S(1)}, bf16[512]{0:T(512)(128)(2,1)S(1)}, u32[]{:S(2)}, u32[]{:S(2)}) collective-permute-start(bf16[512]{0:T(512)(128)(2,1)S(1)} %get-tuple-element.197), channel_id=1, source_target_pairs={{0,1},{1,2},{2,3},{3,4},{4,5},{5,6},{6,7},{7,8},{8,9},{9,10},{10,1... | collective-permute-start | bytes 3080 | tf_op jit(solution)/shard_map/ppermute | solution.py:22
  12.4 66.9 %collective-permute-start.2 = (bf16[512]{0:T(512)(128)(2,1)S(1)}, bf16[512]{0:T(512)(128)(2,1)S(1)}, u32[]{:S(2)}, u32[]{:S(2)}) collective-permute-start(bf16[512]{0:T(512)(128)(2,1)S(1)} %get-tuple-element.197), channel_id=1, source_target_pairs={{0,2},{1,3},{2,4},{3,5},{4,6},{5,7},{6,8},{7,9},{8,10},{9,11},{10,... | collective-permute-start | bytes 3080 | tf_op jit(solution)/shard_map/ppermute | solution.py:22
  64.9 18.3 %collective-permute-start.5 = (bf16[512,768]{1,0:T(8,128)(2,1)}, bf16[512,768]{1,0:T(8,128)(2,1)}, u32[]{:S(2)}, u32[]{:S(2)}) collective-permute-start(bf16[512,768]{1,0:T(8,128)(2,1)} %slice.143), channel_id=1, source_target_pairs={{0,1},{1,2},{2,3},{3,4},{4,5},{5,6},{6,7},{7,8},{8,9},{9,10},{10,1... | collective-permute-start | bytes 2359304 | tf_op jit(solution)/shard_map/ppermute | solution.py:22
  68.4 32.4 %collective-permute-start.4 = (bf16[512,768]{1,0:T(8,128)(2,1)}, bf16[512,768]{1,0:T(8,128)(2,1)}, u32[]{:S(2)}, u32[]{:S(2)}) collective-permute-start(bf16[512,768]{1,0:T(8,128)(2,1)} %slice.143), channel_id=1, source_target_pairs={{0,2},{1,3},{2,4},{3,5},{4,6},{5,7},{6,8},{7,9},{8,10},{9,11},{10,... | collective-permute-start | bytes 2359304 | tf_op jit(solution)/shard_map/ppermute | solution.py:22
  73.7 37.6 %collective-permute-start.1 = (bf16[512,768]{0,1:T(8,128)(2,1)}, bf16[512,768]{0,1:T(8,128)(2,1)}, u32[]{:S(2)}, u32[]{:S(2)}) collective-permute-start(bf16[512,768]{0,1:T(8,128)(2,1)} %bitcast.3), channel_id=1, source_target_pairs={{0,1},{1,2},{2,3},{3,4},{4,5},{5,6},{6,7},{7,8},{8,9},{9,10},{10,1... | collective-permute-start | bytes 2359304 | tf_op jit(solution)/shard_map/ppermute | solution.py:22
  76.1 44.1 %collective-permute-start = (bf16[512,768]{0,1:T(8,128)(2,1)}, bf16[512,768]{0,1:T(8,128)(2,1)}, u32[]{:S(2)}, u32[]{:S(2)}) collective-permute-start(bf16[512,768]{0,1:T(8,128)(2,1)} %bitcast.3), channel_id=1, source_target_pairs={{0,2},{1,3},{2,4},{3,5},{4,6},{5,7},{6,8},{7,9},{8,10},{9,11},{10,... | collective-permute-start | bytes 2359304 | tf_op jit(solution)/shard_map/ppermute | solution.py:22
  263.0 8.9 %copy-start = (f32[12,1536,64]{1,2,0:T(8,128)S(1)}, f32[12,1536,64]{1,2,0:T(8,128)}, u32[]{:S(2)}) copy-start(f32[12,1536,64]{1,2,0:T(8,128)} %get-tuple-element.101) | copy-start | bytes 14155780
  266.0 21.1 %collective-permute-start.7 = (bf16[512,768]{0,1:T(8,128)(2,1)S(1)}, bf16[512,768]{0,1:T(8,128)(2,1)S(1)}, u32[]{:S(2)}, u32[]{:S(2)}) collective-permute-start(bf16[512,768]{0,1:T(8,128)(2,1)S(1)} %bitcast.143), channel_id=1, source_target_pairs={{2,0},{3,1},{4,2},{5,3},{6,4},{7,5},{8,6},{9,7},{10,8},{11,9},{12,... | collective-permute-start | bytes 2359304 | tf_op jit(solution)/shard_map/ppermute | solution.py:22
  270.0 22.7 %collective-permute-start.6 = (bf16[512,768]{0,1:T(8,128)(2,1)S(1)}, bf16[512,768]{0,1:T(8,128)(2,1)S(1)}, u32[]{:S(2)}, u32[]{:S(2)}) collective-permute-start(bf16[512,768]{0,1:T(8,128)(2,1)S(1)} %bitcast.142), channel_id=1, source_target_pairs={{1,0},{2,1},{3,2},{4,3},{5,4},{6,5},{7,6},{8,7},{9,8},{10,9},{11,1... | collective-permute-start | bytes 2359304 | tf_op jit(solution)/shard_map/ppermute | solution.py:22
  274.1 29.8 %collective-permute-start.9 = (bf16[512,768]{0,1:T(8,128)(2,1)S(1)}, bf16[512,768]{0,1:T(8,128)(2,1)S(1)}, u32[]{:S(2)}, u32[]{:S(2)}) collective-permute-start(bf16[512,768]{0,1:T(8,128)(2,1)S(1)} %bitcast.137), channel_id=1, source_target_pairs={{2,0},{3,1},{4,2},{5,3},{6,4},{7,5},{8,6},{9,7},{10,8},{11,9},{12,... | collective-permute-start | bytes 2359304 | tf_op jit(solution)/shard_map/ppermute | solution.py:22
  276.0 17.0 %copy-start.3 = (f32[12,512,64]{1,2,0:T(8,128)S(1)}, f32[12,512,64]{1,2,0:T(8,128)}, u32[]{:S(2)}) copy-start(f32[12,512,64]{1,2,0:T(8,128)} %get-tuple-element.99) | copy-start | bytes 4718596
  276.0 38.4 %collective-permute-start.8 = (bf16[512,768]{0,1:T(8,128)(2,1)S(1)}, bf16[512,768]{0,1:T(8,128)(2,1)S(1)}, u32[]{:S(2)}, u32[]{:S(2)}) collective-permute-start(bf16[512,768]{0,1:T(8,128)(2,1)S(1)} %bitcast.136), channel_id=1, source_target_pairs={{1,0},{2,1},{3,2},{4,3},{5,4},{6,5},{7,6},{8,7},{9,8},{10,9},{11,1... | collective-permute-start | bytes 2359304 | tf_op jit(solution)/shard_map/ppermute | solution.py:22
  293.8 21.0 %copy-start.5 = (bf16[512,12,64]{0,2,1:T(8,128)(2,1)}, bf16[512,12,64]{0,2,1:T(8,128)(2,1)S(1)}, u32[]{:S(2)}) copy-start(bf16[512,12,64]{0,2,1:T(8,128)(2,1)S(1)} %get-tuple-element.223) | copy-start | bytes 2359300
  293.8 21.0 %copy-start.2 = (bf16[512,768]{1,0:T(8,128)(2,1)S(1)}, bf16[512,768]{1,0:T(8,128)(2,1)}, u32[]{:S(2)}) copy-start(bf16[512,768]{1,0:T(8,128)(2,1)} %param.15) | copy-start | bytes 2359300
  314.8 5.2 %copy-start.7 = (bf16[512,768]{0,1:T(8,128)(2,1)}, bf16[512,768]{0,1:T(8,128)(2,1)S(1)}, u32[]{:S(2)}) copy-start(bf16[512,768]{0,1:T(8,128)(2,1)S(1)} %fusion.47) | copy-start | bytes 2359300
  320.0 1.1 copy-start.4
  320.0 2.3 copy-start.6
Sparse Core Ops, SparseCore 0:
  10.3 48.1 all-gather.1
  320.1 88.7 reduce-scatter.1
where the time goes:
time: 422 us; the launch traced here: 418 us
  waiting for transfers between devices  192 us (45%)
  matrix products  137 us (32%)
  other arithmetic  32.1 us (8%)
  starting transfers between devices  28.6 us (7%)
  between operations  14.4 us (3%)
  local copies, waits for them, and re-layouts  13.8 us (3%)
    reduce_scatter x1, waiting for transfers between devices, local(): lax.psum_scatter(jnp.dot(columns.T, dqkv, preferred_element_type=jnp.floa...  80.9 us
    ppermute x10, waiting for transfers between devices, shifted(): lax.ppermute(value, axis, [(source, source + steps) for source in range(l...  70.6 us
    all_gather x1, waiting for transfers between devices, local(): lax.all_gather(projection, 'seq', axis=0, tiled=True)  39.3 us
    ppermute x10, starting transfers between devices, shifted(): lax.ppermute(value, axis, [(source, source + steps) for source in range(l...  28.5 us
    dot_general x12, matrix products, head_block(): value_grad = jnp.dot(probs.T, out_grads, preferred_element_type=jnp.float32)  27.4 us
    dot_general x12, matrix products, head_block(): jnp.dot(probs, value_block, preferred_element_type=jnp.float32)  27.1 us
    dot_general x12, matrix products, head_block(): jnp.dot(out_grads, value_block.T, preferred_element_type=jnp.float32)  20.9 us
    dot_general x12, matrix products, head_block(): jnp.dot(queries, key_block.T, preferred_element_type=jnp.float32)  19 us
  transfers between devices with their start and end apart: 12, of which 10 were waited for; matrix products, arithmetic and copies ran while one was open for 7% of the time, Pallas kernels for 0%

commit v1 on v0

v1 whole, which is shorter than its diff:
```python
import functools
import math

import jax
import jax.numpy as jnp
from jax import lax
from jax.experimental import pallas as pl
from jax.experimental.pallas import tpu as pltpu
from jax.sharding import PartitionSpec as P

D = 768
H = 12
HD = 64
W = 1024
EPSILON = 1e-05
SCORE_SCALE = 0.125
MASKED_SCORE = -1e30
BLOCK = 256
SPAN = BLOCK + W
PAIR = 2 * HD
HALF = D // 2


def contract(a, b, da, db):
    return lax.dot_general(a, b, (((da,), (db,)), ((), ())), preferred_element_type=jnp.float32)


def attention_kernel(
    core_ref, nx_ref, wq_ref, wk_ref, wv_ref, cos_ref, sin_ref, segq_ref, segk_ref, do_ref,
    ctx_ref, dq_ref, dk_ref, dv_ref,
    bias, qs, ks, vs, dka, dva,
):
    own = ctx_ref.shape[0]
    total = nx_ref.shape[0]
    lane = lax.broadcasted_iota(jnp.int32, (1, PAIR), 1)
    low = (lane % HD) < HD // 2

    def swap(u):
        return jnp.where(low, pltpu.roll(u, PAIR - HD // 2, 1), pltpu.roll(u, HD // 2, 1))

    @pl.when(pl.program_id(0) == 0)
    def _():
        row = lax.broadcasted_iota(jnp.int32, (BLOCK, SPAN), 0)
        col = lax.broadcasted_iota(jnp.int32, (BLOCK, SPAN), 1)
        near = (col > row) & (col <= row + W)
        for b in range(own // BLOCK):
            same = segq_ref[b * BLOCK : (b + 1) * BLOCK, :] == segk_ref[:, b * BLOCK : b * BLOCK + SPAN]
            bias[b] = jnp.where(near & same, 0.0, MASKED_SCORE)

    def project(i, carry):
        rows = pl.ds(pl.multiple_of(i * BLOCK, BLOCK), BLOCK)
        x = nx_ref[rows, :]
        k = contract(x, wk_ref[...], 1, 0)
        ks[rows, :] = (k * cos_ref[rows, :] + swap(k) * sin_ref[rows, :]).astype(jnp.bfloat16)
        vs[rows, :] = contract(x, wv_ref[...], 1, 0).astype(jnp.bfloat16)
        dka[rows, :] = jnp.zeros((BLOCK, PAIR), jnp.float32)
        dva[rows, :] = jnp.zeros((BLOCK, PAIR), jnp.float32)
        return carry

    lax.fori_loop(0, total // BLOCK, project, 0)

    def query(i, carry):
        rows = pl.ds(pl.multiple_of(i * BLOCK, BLOCK), BLOCK)
        here = pl.ds(pl.multiple_of(i * BLOCK + W, BLOCK), BLOCK)
        q = contract(nx_ref[here, :], wq_ref[...], 1, 0)
        q = (q * cos_ref[here, :] + swap(q) * sin_ref[here, :]).astype(jnp.bfloat16)
        qs[rows, :] = q * jnp.bfloat16(SCORE_SCALE)
        return carry

    lax.fori_loop(0, own // BLOCK, query, 0)

    def visit(b, carry):
        rows = pl.ds(pl.multiple_of(b * BLOCK, BLOCK), BLOCK)
        here = pl.ds(pl.multiple_of(b * BLOCK + W, BLOCK), BLOCK)
        window = pl.ds(pl.multiple_of(b * BLOCK, BLOCK), SPAN)
        contexts, grads = [], []
        for h in range(2):
            mine = (lane // HD) == h
            kb = ks[window, :]
            vb = vs[window, :]
            qh = jnp.where(mine, qs[rows, :], jnp.bfloat16(0))
            gh = jnp.where(mine, do_ref[rows, :], jnp.bfloat16(0))
            s = contract(qh, kb, 1, 1) + bias[b]
            e = jnp.exp(s - jnp.max(s, axis=1, keepdims=True))
            w = e * (1.0 / jnp.sum(e, axis=1, keepdims=True))
            pb = w.astype(jnp.bfloat16)
            context = contract(pb, vb, 1, 0).astype(jnp.bfloat16)
            delta = jnp.sum(
                gh.astype(jnp.float32) * context.astype(jnp.float32), axis=1, keepdims=True
            )
            dp = contract(gh, vb, 1, 1)
            ds = (w * (dp - delta)).astype(jnp.bfloat16)
            contexts.append(context)
            grads.append(contract(ds, kb, 1, 0))
            dka[window, :] += contract(ds, qh, 0, 0)
            dva[window, :] += contract(pb, gh, 0, 0)
        first = lane < HD
        ctx_ref[rows, :] = jnp.where(first, contexts[0], contexts[1])
        g = jnp.where(first, grads[0], grads[1]) * SCORE_SCALE
        dq_ref[rows, :] = (g * cos_ref[here, :] - swap(g) * sin_ref[here, :]).astype(jnp.bfloat16)
        return carry

    lax.fori_loop(0, own // BLOCK, visit, 0)

    def finish(i, carry):
        rows = pl.ds(pl.multiple_of(i * BLOCK, BLOCK), BLOCK)
        g = dka[rows, :]
        dk_ref[rows, :] = (g * cos_ref[rows, :] - swap(g) * sin_ref[rows, :]).astype(jnp.bfloat16)
        dv_ref[rows, :] = dva[rows, :].astype(jnp.bfloat16)
        return carry

    lax.fori_loop(0, total // BLOCK, finish, 0)


def attention(core, nx, weights, cosine, sine, seg_q, seg_k, out_grads):
    total = nx.shape[0]
    own = total - W
    pairs = HALF // PAIR

    def whole(shape):
        return pl.BlockSpec(shape, lambda p, c: (0, 0))

    def columns(start):
        return pl.BlockSpec((D, PAIR), lambda p, c: (0, start + c[0] * pairs + p))

    def heads(rows):
        return pl.BlockSpec((rows, PAIR), lambda p, c: (0, p))

    return pl.pallas_call(
        attention_kernel,
        out_shape=[
            jax.ShapeDtypeStruct((own, HALF), jnp.bfloat16),
            jax.ShapeDtypeStruct((own, HALF), jnp.bfloat16),
            jax.ShapeDtypeStruct((total, HALF), jnp.bfloat16),
            jax.ShapeDtypeStruct((total, HALF), jnp.bfloat16),
        ],
        grid_spec=pltpu.PrefetchScalarGridSpec(
            num_scalar_prefetch=1,
            grid=(pairs,),
            in_specs=[
                whole((total, D)),
                columns(0),
                columns(2 * pairs),
                columns(4 * pairs),
                whole((total, PAIR)),
                whole((total, PAIR)),
                whole((own, 1)),
                whole((1, total)),
                heads(own),
            ],
            out_specs=[heads(own), heads(own), heads(total), heads(total)],
            scratch_shapes=[
                pltpu.VMEM((own // BLOCK, BLOCK, SPAN), jnp.float32),
                pltpu.VMEM((own, PAIR), jnp.bfloat16),
                pltpu.VMEM((total, PAIR), jnp.bfloat16),
                pltpu.VMEM((total, PAIR), jnp.bfloat16),
                pltpu.VMEM((total, PAIR), jnp.float32),
                pltpu.VMEM((total, PAIR), jnp.float32),
            ],
        ),
        compiler_params=pltpu.CompilerParams(vmem_limit_bytes=48 * 1024 * 1024),
        name="window_attention",
    )(core, nx, weights, weights, weights, cosine, sine, seg_q, seg_k, out_grads)


def swapped(value):
    count = lax.axis_size("seq")
    return lax.ppermute(value, "seq", [(s, s ^ 1) for s in range(count)])


def chip_shifted(value, steps):
    count = lax.axis_size("seq")
    pairs = [(s, s + 2 * steps) for s in range(count) if 0 <= s + 2 * steps < count]
    return lax.ppermute(value, "seq", pairs)


def ordered(core, mine, other, axis=0):
    first = jnp.where(core == 0, mine, other)
    second = jnp.where(core == 0, other, mine)
    return jnp.concatenate([first, second], axis=axis)


def local(inputs, projection, positions, segments, context_grad):
    row_count = inputs.shape[0]
    device_count = lax.axis_size("seq")
    chips = device_count // 2
    device_index = lax.axis_index("seq")
    core = device_index % 2
    chip = device_index // 2
    assert 2 * row_count == W
    grad_scale = (row_count * device_count) ** (-0.5)

    weights = lax.all_gather(projection, "seq", axis=0, tiled=True)

    meta = jnp.stack([positions, segments], axis=0)
    x_before = chip_shifted(inputs, 1)
    meta_before = chip_shifted(meta, 1)
    x_other = swapped(inputs)
    meta_other = swapped(meta)
    x_before_other = swapped(x_before)
    meta_before_other = swapped(meta_before)
    grad_mine = lax.dynamic_slice_in_dim(context_grad, core * HALF, HALF, 1)
    grad_sent = lax.dynamic_slice_in_dim(context_grad, (1 - core) * HALF, HALF, 1)
    grad_other = swapped(grad_sent)
    out_grads = ordered(core, grad_mine, grad_other)

    x_all = jnp.concatenate(
        [ordered(core, x_before, x_before_other), ordered(core, inputs, x_other)], axis=0
    ).astype(jnp.float32)
    nx = (
        x_all * lax.rsqrt(jnp.mean(x_all * x_all, axis=1, keepdims=True) + EPSILON)
    ).astype(jnp.bfloat16)
    meta_all = jnp.concatenate(
        [ordered(core, meta_before, meta_before_other, 1), ordered(core, meta, meta_other, 1)],
        axis=1,
    )
    half_size = HD // 2
    frequency = jnp.exp(-math.log(10000.0) * jnp.arange(half_size, dtype=jnp.float32) / half_size)
    angle = meta_all[0].astype(jnp.float32)[:, None] * frequency[None, :]
    c, s = jnp.cos(angle), jnp.sin(angle)
    cosine = jnp.concatenate([c, c, c, c], axis=1)
    sine = jnp.concatenate([-s, s, -s, s], axis=1)
    seg_all = meta_all[1]
    outside = (jnp.arange(seg_all.shape[0]) < W) & (chip == 0)
    seg_k = jnp.where(outside, -1, seg_all)[None, :]
    seg_q = seg_all[W:][:, None]

    context_heads, dq, dk, dv = attention(
        core.astype(jnp.int32)[None], nx, weights, cosine, sine, seg_q, seg_k, out_grads
    )

    mine_at = core * row_count
    other_at = (1 - core) * row_count
    context_mine = lax.dynamic_slice_in_dim(context_heads, mine_at, row_count, 0)
    context_other = swapped(lax.dynamic_slice_in_dim(context_heads, other_at, row_count, 0))
    context = ordered(core, context_mine, context_other, 1)

    w_q, w_k, w_v = [
        lax.dynamic_slice_in_dim(weights, t * D + core * HALF, HALF, 1) for t in range(3)
    ]
    dkv = jnp.concatenate([dk, dv], axis=1)
    w_kv = jnp.concatenate([w_k, w_v], axis=1)
    ng_kv = contract(dkv, w_kv, 1, 1)
    ng_q = contract(dq, w_q, 1, 1)
    ng_before = ng_kv[:W]
    ng_own = ng_kv[W:] + ng_q
    send_before = lax.dynamic_slice_in_dim(ng_before, other_at, row_count, 0).astype(jnp.bfloat16)
    keep_before = lax.dynamic_slice_in_dim(ng_before, mine_at, row_count, 0)
    before = keep_before + swapped(send_before).astype(jnp.float32)
    later = chip_shifted(before.astype(jnp.bfloat16), -1)
    send_own = lax.dynamic_slice_in_dim(ng_own, other_at, row_count, 0).astype(jnp.bfloat16)
    keep_own = lax.dynamic_slice_in_dim(ng_own, mine_at, row_count, 0)
    normed_grad = (
        keep_own + swapped(send_own).astype(jnp.float32) + later.astype(jnp.float32)
    )
    x_float = inputs.astype(jnp.float32)
    inv_rms = lax.rsqrt(jnp.mean(x_float * x_float, axis=1, keepdims=True) + EPSILON)
    scaled = x_float * inv_rms
    input_grad = (
        inv_rms * (normed_grad - scaled * jnp.mean(normed_grad * scaled, axis=1, keepdims=True))
    ).astype(jnp.bfloat16)

    pg_kv = contract(nx, dkv, 0, 0)
    pg_q = contract(nx[W:], dq, 0, 0)
    pg = jnp.concatenate([pg_q, pg_kv], axis=1).astype(jnp.bfloat16)
    groups = [[2 * i + k for i in range(chips)] for k in range(2)]
    summed = lax.psum_scatter(
        pg, "seq", scatter_dimension=0, axis_index_groups=groups, tiled=True
    ).astype(jnp.float32)
    rows = summed.shape[0] // 2
    keep = lax.dynamic_slice_in_dim(summed, core * rows, rows, 0)
    other = swapped(lax.dynamic_slice_in_dim(summed, (1 - core) * rows, rows, 0).astype(jnp.bfloat16))
    other = other.astype(jnp.float32)
    parts = []
    for t in range(3):
        cols = slice(t * HALF, (t + 1) * HALF)
        parts.append(ordered(core, keep[:, cols], other[:, cols], 1))
    projection_grad = jnp.concatenate(parts, axis=1) * grad_scale
    return (context, input_grad, projection_grad)


def solution(mesh):
    in_specs = (
        P(("groups", "seq"), None),
        P("seq", None),
        P(("groups", "seq")),
        P(("groups", "seq")),
        P(("groups", "seq"), None),
    )
    out_specs = (P(("groups", "seq"), None), P(("groups", "seq"), None), P(("groups", "seq"), None))
    return jax.shard_map(local, mesh=mesh, in_specs=in_specs, out_specs=out_specs, check_vma=False)
```

time: 422 us -> 225 us (0.53)
  matrix products: 137 us -> 9.36 us
  waiting for transfers between devices: 192 us -> 78.9 us
  Pallas kernels: 0 us -> 57.9 us
  starting transfers between devices: 28.6 us -> 15.4 us
  local copies, waits for them, and re-layouts: 13.8 us -> 22.4 us
  other arithmetic: 32.1 us -> 25 us
    dot_general x75 -> x4, matrix products: 137 us -> 9.36 us  [contract(): lax.dot_general(a, b, (((da,), (db,)), ((), ())), preferred_element_type=...]
    reduce_scatter x1 -> x0, waiting for transfers between devices: 80.9 us -> none  [local(): lax.psum_scatter(jnp.dot(columns.T, dqkv, preferred_element_type=jnp.floa...]
    pallas_call x0 -> x1, Pallas kernels: none -> 57.9 us  [attention(): pl.pallas_call(attention_kernel, out_shape=[jax.ShapeDtypeStruct((own, HA...]
    ppermute x10 -> x12, waiting for transfers between devices: 70.6 us -> 38.7 us  [the longest x3 37.7 us: chip_shifted(): return lax.ppermute(value, 'seq', pairs)]
    unnamed x2 -> x3, waiting for transfers between devices: 0.7 us -> 29.5 us
    all_gather x1, waiting for transfers between devices: 39.3 us -> 10.7 us  [local(): weights = lax.all_gather(projection, 'seq', axis=0, tiled=True)]
    reduce_sum x24 -> x2, other arithmetic: 17.4 us -> 3.14 us  [the longest x1 2.17 us: local(): jnp.mean(normed_grad * scaled, axis=1, keepdims=True)]
    ppermute x10 -> x12, starting transfers between devices: 28.5 us -> 15.3 us  [the longest x3 9.4 us: chip_shifted(): return lax.ppermute(value, 'seq', pairs)]
  transfers between devices with their start and end apart: 12 -> 14, of which waited for: 10 -> 6; matrix products, arithmetic and copies ran while one was open for 7% -> 16% of each run, Pallas kernels for 0% -> 0%
where the time goes in v1:
time: 225 us; the launch traced here: 223 us
  waiting for transfers between devices  78.9 us (35%)
  Pallas kernels  57.9 us (26%)
  other arithmetic  25 us (11%)
  local copies, waits for them, and re-layouts  22.4 us (10%)
  starting transfers between devices  15.4 us (7%)
  between operations  14.5 us (6%)
  matrix products  9.36 us (4%)
    pallas_call x1, Pallas kernels, attention(): pl.pallas_call(attention_kernel, out_shape=[jax.ShapeDtypeStruct((own, HA...  57.9 us
    ppermute x3, waiting for transfers between devices, chip_shifted(): return lax.ppermute(value, 'seq', pairs)  37.7 us
    unnamed x3, waiting for transfers between devices  29.5 us
    unnamed x48, local copies, waits for them, and re-layouts  16.2 us
    all_gather x1, waiting for transfers between devices, local(): weights = lax.all_gather(projection, 'seq', axis=0, tiled=True)  10.7 us
    ppermute x3, starting transfers between devices, chip_shifted(): return lax.ppermute(value, 'seq', pairs)  9.4 us
    dot_general x4, matrix products, contract(): lax.dot_general(a, b, (((da,), (db,)), ((), ())), preferred_element_type=...  9.36 us
    ppermute x9, starting transfers between devices, swapped(): return lax.ppermute(value, 'seq', [(s, s ^ 1) for s in range(count)])  5.93 us
  transfers between devices with their start and end apart: 14, of which 6 were waited for; matrix products, arithmetic and copies ran while one was open for 16% of the time, Pallas kernels for 0%

profile of v1, /device:TPU:11, one launch (start us, length us, event | category | flops | bytes accessed | tf_op | source)
XLA Modules:
  0.0 223.4 jit_solution(11533130522122529957)
XLA Ops:
  7.2 0.7 all-gather.2.cloned.1.call-update
  7.9 0.7 pad_add_fusion.2
  8.7 3.2 %collective-permute-start.3 = (s32[2,512]{1,0:T(2,128)S(1)}, s32[2,512]{1,0:T(2,128)S(1)}, u32[]{:S(2)}, u32[]{:S(2)}) collective-permute-start(s32[2,512]{1,0:T(2,128)S(1)} %pad_add_fusion.2), channel_id=1, source_target_pairs={{0,2},{1,3},{2,4},{3,5},{4,6},{5,7},{6,8},{7,9},{8,10},{9,11},{10,... | collective-permute-start | bytes 12296 | tf_op jit(solution)/shard_map/ppermute | solution.py:174
  11.8 1.0 collective-permute-start.5
  12.8 3.1 %collective-permute-start = (bf16[512,768]{1,0:T(8,128)(2,1)}, bf16[512,768]{1,0:T(8,128)(2,1)}, u32[]{:S(2)}, u32[]{:S(2)}) collective-permute-start(bf16[512,768]{1,0:T(8,128)(2,1)} %param.5), channel_id=1, source_target_pairs={{0,2},{1,3},{2,4},{3,5},{4,6},{5,7},{6,8},{7,9},{8,10},{9,11},{10,... | collective-permute-start | bytes 2359304 | tf_op jit(solution)/shard_map/ppermute | solution.py:174
  16.0 0.4 collective-permute-start.2
  16.3 1.0 constant_dynamic-slice_fusion.3
  18.0 0.7 broadcast_select_fusion.9
  19.2 3.7 %fusion.19 = (f32[2048,32]{1,0:T(8,128)S(1)}, f32[2048,32]{1,0:T(8,128)S(1)}, f32[2048,32]{1,0:T(8,128)S(1)}) fusion(f32[32]{0:T(128)S(1)} %multiply_exponential_fusion, f32[2048]{0:T(1024)S(1)} %bitcast.12), kind=kLoop, calls=%fused_computation.44 | loop fusion | flops 131072 | bytes 794752 | tf_op jit(solution)/shard_map/neg | solution.py:222
  22.9 17.4 %collective-permute-done = bf16[512,768]{1,0:T(8,128)(2,1)} collective-permute-done((bf16[512,768]{1,0:T(8,128)(2,1)}, bf16[512,768]{1,0:T(8,128)(2,1)}, u32[]{:S(2)}, u32[]{:S(2)}) %collective-permute-start) | collective-permute-done | bytes 786464 | tf_op jit(solution)/shard_map/ppermute | solution.py:174
  40.3 0.8 collective-permute-start.1
  41.1 1.7 pad_maximum_fusion.2
  43.1 1.3 broadcast_select_fusion.1
  44.5 1.3 broadcast_select_fusion.3
  45.8 1.0 fusion
  46.8 4.1 %fusion.1.nx_ref = bf16[2048,768]{1,0:T(8,128)(2,1)} fusion(f32[2048]{0:T(1024)S(1)} %add_rsqrt_fusion, bf16[512,768]{1,0:T(8,128)(2,1)S(1)} %get-tuple-element.28, bf16[512,768]{1,0:T(8,128)(2,1)S(1)} %get-tuple-element.27, bf16[512,768]{1,0:T(8,128)(2,1)S(1)} %get-tuple-element.26, bf16[512,768]{1,0:T(8,128)(2,1)S(1)} %get-tuple-element.25), kind=kLoop, calls=%fused_computation.3 | loop fusion | flops 15728640 | bytes 6299648 | tf_op jit(solution)/shard_map/convert_element_type | solution.py:212
  50.9 10.7 %all-gather.2.cloned.1.call-done.wq_ref.wk_ref.wv_ref = bf16[768,2304]{1,0:T(8,128)(2,1)} async-done(((bf16[48,2304]{1,0:T(8,128)(2,1)}), bf16[768,2304]{1,0:T(8,128)(2,1)}) %all-gather.2.cloned.1.call-update) | async-done | bytes 3538960 | tf_op jit(solution)/shard_map/all_gather | solution.py:193
  61.6 57.9 %window_attention.1 = (bf16[1024,384]{1,0:T(8,128)(2,1)S(1)}, bf16[1024,384]{1,0:T(8,128)(2,1)S(1)}, bf16[2048,384]{1,0:T(8,128)(2,1)}, bf16[2048,384]{1,0:T(8,128)(2,1)}) custom-call(s32[1]{0:T(128)} %bitcast.core_ref, bf16[2048,768]{1,0:T(8,128)(2,1)} %fusion.1.nx_ref, bf16[768,2304]{1,0:T(8,128)(2,1)} %all-gather.2.cloned.1.call-done.wq_ref.wk_ref.wv_ref, ...), custom_call_target="tpu_custom_call" | custom-call | tf_op jit(solution)/shard_map/window_attention/pallas_call | solution.py:129
  119.5 2.2 constant_dynamic-update-slice_fusion.1
  122.2 0.6 copy-done.7
  122.9 2.7 %convolution_convert_fusion = bf16[768,768]{0,1:T(8,128)(2,1)S(1)} fusion(bf16[2048,768]{1,0:T(8,128)(2,1)S(1)} %copy-done.7, bf16[2048,768]{1,0:T(8,128)(2,1)S(1)} %constant_dynamic-update-slice_fusion), kind=kOutput, calls=%fused_computation.22 | convolution fusion | flops 2416508928 | bytes 7471104 | tf_op jit(solution)/shard_map/dot_general | solution.py:25
  125.6 0.8 fusion.11
  126.5 2.2 copy.34
  128.8 1.5 constant_dynamic-slice_fusion.1
  130.3 0.7 copy-done.17
  131.0 2.6 %fusion.14 = f32[2048,768]{0,1:T(8,128)S(1)} fusion(bf16[2048,768]{1,0:T(8,128)(2,1)S(1)} %copy-done.17, bf16[768,384]{1,0:T(8,128)(2,1)S(1)} %get-tuple-element.24, bf16[768,384]{1,0:T(8,128)(2,1)S(1)} %get-tuple-element.23), kind=kOutput, calls=%fused_computation.26 | convolution fusion | flops 2418278400 | bytes 10616832 | tf_op jit(solution)/shard_map/dot_general | solution.py:25
  133.7 0.4 slice.54
  134.0 2.2 copy-done.11
  136.3 1.7 copy-done.9
  138.5 3.2 %slice_add_fusion = f32[1024,768]{0,1:T(8,128)S(1)} fusion(f32[2048,768]{0,1:T(8,128)} %copy-done.11, bf16[1024,384]{1,0:T(8,128)(2,1)S(1)} %copy-done.1, bf16[768,2304]{1,0:T(8,128)(2,1)} %all-gather.2.cloned.1.call-done.wq_ref.wk_ref.wv_ref, s32[]{:T(128)S(6)} %select_n.159), kind=kOutput, calls=%fused_computation.4 | convolution fusion | flops 604766208 | bytes 7667716 | tf_op jit(solution)/shard_map/dot_general | solution.py:25
  141.7 1.6 copy-done.4
  143.4 1.0 dynamic-slice_convert_fusion.1
  144.6 1.2 add_convert_fusion
  145.8 3.1 %collective-permute-start.10 = (bf16[512,768]{0,1:T(8,128)(2,1)}, bf16[512,768]{0,1:T(8,128)(2,1)}, u32[]{:S(2)}, u32[]{:S(2)}) collective-permute-start(bf16[512,768]{0,1:T(8,128)(2,1)} %add_convert_fusion), channel_id=1, source_target_pairs={{2,0},{3,1},{4,2},{5,3},{6,4},{7,5},{8,6},{9,7},{10,8},{11,9},{12,... | collective-permute-start | bytes 2359304 | tf_op jit(solution)/shard_map/ppermute | solution.py:174
  149.0 0.6 collective-permute-start.7
  150.2 0.8 collective-permute-done.7
  151.2 0.9 pad_maximum_fusion.5
  152.1 20.4 %collective-permute-done.10 = bf16[512,768]{0,1:T(8,128)(2,1)} collective-permute-done((bf16[512,768]{0,1:T(8,128)(2,1)}, bf16[512,768]{0,1:T(8,128)(2,1)}, u32[]{:S(2)}, u32[]{:S(2)}) %collective-permute-start.10) | collective-permute-done | bytes 786464 | tf_op jit(solution)/shard_map/ppermute | solution.py:174
  172.5 2.2 fusion.4
  174.7 28.8 %reduce-scatter.4.cloned.1.call-done = bf16[96,1152]{1,0:T(8,128)(2,1)} async-done(((bf16[768,1152]{1,0:T(8,128)(2,1)}), bf16[96,1152]{1,0:T(8,128)(2,1)}) %reduce-scatter.4.cloned.1.call-update) | async-done | bytes 221200
  203.5 1.1 copy.35
  204.7 0.8 copy-done.12
  205.5 0.9 dynamic-slice_convert_fusion.2
  206.4 1.9 collective-permute-start.11
  208.3 3.0 %fusion.7 = bf16[512,768]{0,1:T(8,128)(2,1)} fusion(bf16[512,768]{0,1:T(8,128)(2,1)} %copy-done.8, f32[512]{0:T(512)S(1)} %broadcast_multiply_fusion.1, f32[512]{0:T(512)S(1)} %add_rsqrt_fusion.1, bf16[512,768]{0,1:T(8,128)(2,1)} %collective-permute-done.10, bf16[512,768]{0,1:T(8,128)(2,1)} %collective-permute-done.8, f32[1024,768]{0,1:T(8,128)S(1)} %copy-done.6, ...), kind=kLoop, calls=%fused_computation.14 | loop fusion | flops 3932160 | bytes 4722692 | tf_op jit(solution)/shard_map/convert_element_type | solution.py:261
  211.3 2.3 %copy.33 = bf16[512,768]{1,0:T(8,128)(2,1)} copy(bf16[512,768]{0,1:T(8,128)(2,1)} %fusion.7) | data formatting | bytes 1572864
  213.6 1.3 slice_select_fusion
  215.8 0.8 broadcast_multiply_fusion
  (80 shorter events, 4.5 us)
Async XLA Ops:
  7.2 54.4 %all-gather.2.cloned.1.call-start = ((), (), s32[]{:S(2)}) async-start(), calls=%async_computation.1 | async-start | bytes 3760128 | tf_op jit(solution)/shard_map/all_gather | solution.py:193
  7.9 195.6 %reduce-scatter.4.cloned.1.call-start = ((), (), s32[]{:S(2)}) async-start(), calls=%async_computation.2 | async-start | bytes 1990656
  8.7 9.0 %collective-permute-start.3 = (s32[2,512]{1,0:T(2,128)S(1)}, s32[2,512]{1,0:T(2,128)S(1)}, u32[]{:S(2)}, u32[]{:S(2)}) collective-permute-start(s32[2,512]{1,0:T(2,128)S(1)} %pad_add_fusion.2), channel_id=1, source_target_pairs={{0,2},{1,3},{2,4},{3,5},{4,6},{5,7},{6,8},{7,9},{8,10},{9,11},{10,... | collective-permute-start | bytes 12296 | tf_op jit(solution)/shard_map/ppermute | solution.py:174
  11.8 6.2 %collective-permute-start.5 = (s32[2,512]{1,0:T(2,128)S(1)}, s32[2,512]{1,0:T(2,128)S(1)}, u32[]{:S(2)}, u32[]{:S(2)}) collective-permute-start(s32[2,512]{1,0:T(2,128)S(1)} %pad_add_fusion.2), channel_id=1, source_target_pairs={{0,1},{1,0},{2,3},{3,2},{4,5},{5,4},{6,7},{7,6},{8,9},{9,8},{10,11... | collective-permute-start | bytes 12296 | tf_op jit(solution)/shard_map/ppermute | solution.py:168
  12.8 27.5 %collective-permute-start = (bf16[512,768]{1,0:T(8,128)(2,1)}, bf16[512,768]{1,0:T(8,128)(2,1)}, u32[]{:S(2)}, u32[]{:S(2)}) collective-permute-start(bf16[512,768]{1,0:T(8,128)(2,1)} %param.5), channel_id=1, source_target_pairs={{0,2},{1,3},{2,4},{3,5},{4,6},{5,7},{6,8},{7,9},{8,10},{9,11},{10,... | collective-permute-start | bytes 2359304 | tf_op jit(solution)/shard_map/ppermute | solution.py:174
  16.0 27.2 %collective-permute-start.2 = (bf16[512,768]{1,0:T(8,128)(2,1)}, bf16[512,768]{1,0:T(8,128)(2,1)}, u32[]{:S(2)}, u32[]{:S(2)}) collective-permute-start(bf16[512,768]{1,0:T(8,128)(2,1)} %param.5), channel_id=1, source_target_pairs={{0,1},{1,0},{2,3},{3,2},{4,5},{5,4},{6,7},{7,6},{8,9},{9,8},{10,11... | collective-permute-start | bytes 2359304 | tf_op jit(solution)/shard_map/ppermute | solution.py:168
  17.4 25.4 %collective-permute-start.6 = (bf16[512,384]{1,0:T(8,128)(2,1)S(1)}, bf16[512,384]{1,0:T(8,128)(2,1)S(1)}, u32[]{:S(2)}, u32[]{:S(2)}) collective-permute-start(bf16[512,384]{1,0:T(8,128)(2,1)S(1)} %constant_dynamic-slice_fusion.3), channel_id=1, source_target_pairs={{0,1},{1,0},{2,3},{3,2},{4,5},{5,4},{6,7},{7,6},{8,9},{9,8},{10,11... | collective-permute-start | bytes 1179656 | tf_op jit(solution)/shard_map/ppermute | solution.py:168
  17.7 1.5 collective-permute-start.4
  22.9 19.9 %copy-start.18 = (bf16[512,768]{1,0:T(8,128)(2,1)S(1)}, bf16[512,768]{1,0:T(8,128)(2,1)}, u32[]{:S(2)}) copy-start(bf16[512,768]{1,0:T(8,128)(2,1)} %param.9) | copy-start | bytes 2359300
  40.3 4.2 %collective-permute-start.1 = (bf16[512,768]{1,0:T(8,128)(2,1)}, bf16[512,768]{1,0:T(8,128)(2,1)S(1)}, u32[]{:S(2)}, u32[]{:S(2)}) collective-permute-start(bf16[512,768]{1,0:T(8,128)(2,1)} %collective-permute-done), channel_id=1, source_target_pairs={{0,1},{1,0},{2,3},{3,2},{4,5},{5,4},{6,7},{7,6},{8,9},{9,8},{10,11... | collective-permute-start | bytes 2359304 | tf_op jit(solution)/shard_map/ppermute | solution.py:168
  41.1 2.0 copy-start.13
  119.5 2.8 %copy-start.2 = (bf16[1024,384]{1,0:T(8,128)(2,1)}, bf16[1024,384]{1,0:T(8,128)(2,1)S(1)}, u32[]{:S(2)}) copy-start(bf16[1024,384]{1,0:T(8,128)(2,1)S(1)} %get-tuple-element.7) | copy-start | bytes 2359300
  119.5 6.1 %copy-start = (bf16[1024,384]{1,0:T(8,128)(2,1)}, bf16[1024,384]{1,0:T(8,128)(2,1)S(1)}, u32[]{:S(2)}) copy-start(bf16[1024,384]{1,0:T(8,128)(2,1)S(1)} %get-tuple-element.10) | copy-start | bytes 2359300
  119.5 2.4 %copy-start.15 = (bf16[2048,384]{1,0:T(8,128)(2,1)S(1)}, bf16[2048,384]{1,0:T(8,128)(2,1)}, u32[]{:S(2)}) copy-start(bf16[2048,384]{1,0:T(8,128)(2,1)} %get-tuple-element.9) | copy-start | bytes 4718596
  119.5 3.4 %copy-start.7 = (bf16[2048,768]{1,0:T(8,128)(2,1)S(1)}, bf16[2048,768]{1,0:T(8,128)(2,1)}, u32[]{:S(2)}) copy-start(bf16[2048,768]{1,0:T(8,128)(2,1)} %fusion.1.nx_ref) | copy-start | bytes 9437188
  122.9 2.7 %copy-start.16 = (bf16[2048,768]{1,0:T(8,128)(2,1)}, bf16[2048,768]{1,0:T(8,128)(2,1)S(1)}, u32[]{:S(2)}) copy-start(bf16[2048,768]{1,0:T(8,128)(2,1)S(1)} %constant_dynamic-update-slice_fusion) | copy-start | bytes 9437188
  128.7 2.3 %copy-start.17 = (bf16[2048,768]{1,0:T(8,128)(2,1)S(1)}, bf16[2048,768]{1,0:T(8,128)(2,1)}, u32[]{:S(2)}) copy-start(bf16[2048,768]{1,0:T(8,128)(2,1)} %copy-done.16) | copy-start | bytes 9437188
  133.6 2.6 %copy-start.11 = (f32[2048,768]{0,1:T(8,128)}, f32[2048,768]{0,1:T(8,128)S(1)}, u32[]{:S(2)}) copy-start(f32[2048,768]{0,1:T(8,128)S(1)} %fusion.14) | copy-start | bytes 18874372
  133.6 4.8 %copy-start.1 = (bf16[1024,384]{1,0:T(8,128)(2,1)S(1)}, bf16[1024,384]{1,0:T(8,128)(2,1)}, u32[]{:S(2)}) copy-start(bf16[1024,384]{1,0:T(8,128)(2,1)} %copy-done) | copy-start | bytes 2359300
  136.3 1.7 copy-start.9
  138.1 6.5 %collective-permute-start.9 = (bf16[512,768]{0,1:T(8,128)(2,1)S(1)}, bf16[512,768]{0,1:T(8,128)(2,1)S(1)}, u32[]{:S(2)}, u32[]{:S(2)}) collective-permute-start(bf16[512,768]{0,1:T(8,128)(2,1)S(1)} %dynamic-slice_convert_fusion), channel_id=1, source_target_pairs={{0,1},{1,0},{2,3},{3,2},{4,5},{5,4},{6,7},{7,6},{8,9},{9,8},{10,11... | collective-permute-start | bytes 2359304 | tf_op jit(solution)/shard_map/ppermute | solution.py:168
  138.5 6.2 %copy-start.10 = (f32[1024,768]{0,1:T(8,128)S(1)}, f32[1024,768]{0,1:T(8,128)}, u32[]{:S(2)}) copy-start(f32[1024,768]{0,1:T(8,128)} %copy-done.9) | copy-start | bytes 9437188
  141.7 1.6 copy-start.4
  143.4 5.6 %copy-start.3 = (bf16[1024,384]{1,0:T(8,128)(2,1)S(1)}, bf16[1024,384]{1,0:T(8,128)(2,1)}, u32[]{:S(2)}) copy-start(bf16[1024,384]{1,0:T(8,128)(2,1)} %copy-done.2) | copy-start | bytes 2359300
  143.4 6.3 %copy-start.14 = (bf16[512,768]{1,0:T(8,128)(2,1)S(1)}, bf16[512,768]{1,0:T(8,128)(2,1)}, u32[]{:S(2)}) copy-start(bf16[512,768]{1,0:T(8,128)(2,1)} %param.5) | copy-start | bytes 2359300
  144.4 7.7 %collective-permute-start.8 = (bf16[512,768]{0,1:T(8,128)(2,1)}, bf16[512,768]{0,1:T(8,128)(2,1)}, u32[]{:S(2)}, u32[]{:S(2)}) collective-permute-start(bf16[512,768]{0,1:T(8,128)(2,1)} %dynamic-slice_convert_fusion.1), channel_id=1, source_target_pairs={{0,1},{1,0},{2,3},{3,2},{4,5},{5,4},{6,7},{7,6},{8,9},{9,8},{10,11... | collective-permute-start | bytes 2359304 | tf_op jit(solution)/shard_map/ppermute | solution.py:168
  145.8 26.7 %collective-permute-start.10 = (bf16[512,768]{0,1:T(8,128)(2,1)}, bf16[512,768]{0,1:T(8,128)(2,1)}, u32[]{:S(2)}, u32[]{:S(2)}) collective-permute-start(bf16[512,768]{0,1:T(8,128)(2,1)} %add_convert_fusion), channel_id=1, source_target_pairs={{2,0},{3,1},{4,2},{5,3},{6,4},{7,5},{8,6},{9,7},{10,8},{11,9},{12,... | collective-permute-start | bytes 2359304 | tf_op jit(solution)/shard_map/ppermute | solution.py:174
  149.0 1.9 collective-permute-start.7
  149.9 1.3 copy-start.8
  149.9 22.6 %copy-start.5 = (f32[1024,768]{0,1:T(8,128)S(1)}, f32[1024,768]{0,1:T(8,128)}, u32[]{:S(2)}) copy-start(f32[1024,768]{0,1:T(8,128)} %copy-done.4) | copy-start | bytes 9437188
  152.1 56.2 %copy-start.6 = (f32[1024,768]{0,1:T(8,128)S(1)}, f32[1024,768]{0,1:T(8,128)}, u32[]{:S(2)}) copy-start(f32[1024,768]{0,1:T(8,128)} %copy-done.4) | copy-start | bytes 9437188
  204.7 0.8 copy-start.12
  206.4 7.2 %collective-permute-start.11 = (bf16[48,1152]{0,1:T(8,128)(2,1)}, bf16[48,1152]{0,1:T(8,128)(2,1)S(1)}, u32[]{:S(2)}, u32[]{:S(2)}) collective-permute-start(bf16[48,1152]{0,1:T(8,128)(2,1)} %dynamic-slice_convert_fusion.2), channel_id=1, source_target_pairs={{0,1},{1,0},{2,3},{3,2},{4,5},{5,4},{6,7},{7,6},{8,9},{9,8},{10,11... | collective-permute-start | bytes 331784 | tf_op jit(solution)/shard_map/ppermute | solution.py:168
Sparse Core Ops, SparseCore 0:
  10.3 51.2 all-gather.1
  128.9 74.5 reduce-scatter.3

commit v2 on v1

--- a/solution.py
+++ b/solution.py
@@ -25,20 +25,24 @@
     return lax.dot_general(a, b, (((da,), (db,)), ((), ())), preferred_element_type=jnp.float32)
 
 
-def attention_kernel(
-    core_ref, nx_ref, wq_ref, wk_ref, wv_ref, cos_ref, sin_ref, segq_ref, segk_ref, do_ref,
-    ctx_ref, dq_ref, dk_ref, dv_ref,
+def swap_halves(u, lane):
+    low = (lane % HD) < HD // 2
+    return jnp.where(low, pltpu.roll(u, PAIR - HD // 2, 1), pltpu.roll(u, HD // 2, 1))
+
+
+def pair_attention(
+    p, nx_ref, wq_ref, wk_ref, wv_ref, cos_ref, sin_ref, segq_ref, segk_ref, do_ref,
+    ctx_ref, dq_ref,
     bias, qs, ks, vs, dka, dva,
 ):
     own = ctx_ref.shape[0]
     total = nx_ref.shape[0]
     lane = lax.broadcasted_iota(jnp.int32, (1, PAIR), 1)
-    low = (lane % HD) < HD // 2
 
     def swap(u):
-        return jnp.where(low, pltpu.roll(u, PAIR - HD // 2, 1), pltpu.roll(u, HD // 2, 1))
-
-    @pl.when(pl.program_id(0) == 0)
+        return swap_halves(u, lane)
+
+    @pl.when(p == 0)
     def _():
         row = lax.broadcasted_iota(jnp.int32, (BLOCK, SPAN), 0)
         col = lax.broadcasted_iota(jnp.int32, (BLOCK, SPAN), 1)
@@ -101,6 +105,23 @@
         return carry
 
     lax.fori_loop(0, own // BLOCK, visit, 0)
+
+
+def attention_kernel(
+    core_ref, nx_ref, wq_ref, wk_ref, wv_ref, cos_ref, sin_ref, segq_ref, segk_ref, do_ref,
+    ctx_ref, dq_ref, dk_ref, dv_ref,
+    bias, qs, ks, vs, dka, dva,
+):
+    total = nx_ref.shape[0]
+    lane = lax.broadcasted_iota(jnp.int32, (1, PAIR), 1)
+
+    def swap(u):
+        return swap_halves(u, lane)
+
+    pair_attention(
+        pl.program_id(0), nx_ref, wq_ref, wk_ref, wv_ref, cos_ref, sin_ref, segq_ref, segk_ref,
+        do_ref, ctx_ref, dq_ref, bias, qs, ks, vs, dka, dva,
+    )
 
     def finish(i, carry):
         rows = pl.ds(pl.multiple_of(i * BLOCK, BLOCK), BLOCK)
@@ -163,6 +184,265 @@
     )(core, nx, weights, weights, weights, cosine, sine, seg_q, seg_k, out_grads)
 
 
+def fused_kernel(
+    nx_ref, wq_ref, wk_ref, wv_ref, cos_ref, sin_ref, segq_ref, segk_ref, do_ref,
+    ctx_ref, ng_ref, pg_ref,
+    bias, qs, ks, vs, dka, dva, dqs, dkv, ctxs, ctxr, acc, part, sums, xs, xr, ys, yr, fwd, later,
+    part_send, part_recv, ctx_send, ctx_recv, x_send, x_recv, fwd_send, fwd_recv,
+    *, count, grad_scale,
+):
+    p = pl.program_id(0)
+    last = pl.num_programs(0) - 1
+    me = lax.axis_index("seq")
+    core = lax.rem(me, 2)
+    partner = me + 1 - 2 * core
+    total = nx_ref.shape[0]
+    own = total - W
+    half = own // 2
+    share = D // count
+    chunks = xs.shape[0]
+    piece = half // chunks
+    mine_at = pl.multiple_of(core * half, half)
+    other_at = pl.multiple_of((1 - core) * half, half)
+
+    def remote(source, target, send, recv, device):
+        return pltpu.make_async_remote_copy(
+            src_ref=source, dst_ref=target, send_sem=send, recv_sem=recv,
+            device_id={"seq": device}, device_id_type=pl.DeviceIdType.MESH,
+        )
+
+    @pl.when(p == 0)
+    def _():
+        barrier = pltpu.get_barrier_semaphore()
+
+        def greet(i, carry):
+            pl.semaphore_signal(
+                barrier, inc=1, device_id={"seq": lax.rem(me + 1 + i, count)},
+                device_id_type=pl.DeviceIdType.MESH,
+            )
+            return carry
+
+        lax.fori_loop(0, count - 1, greet, 0)
+        pl.semaphore_wait(barrier, count - 1)
+
+    pair_attention(
+        p, nx_ref, wq_ref, wk_ref, wv_ref, cos_ref, sin_ref, segq_ref, segk_ref, do_ref,
+        ctxs.at[p], dqs, bias, qs, ks, vs, dka, dva,
+    )
+
+    def ctx_copy(pair):
+        return remote(
+            ctxs.at[pair, pl.ds(other_at, half), :], ctxr.at[pair],
+            ctx_send.at[pair], ctx_recv.at[pair], partner,
+        )
+
+    ctx_copy(p).start()
+
+    lane = lax.broadcasted_iota(jnp.int32, (1, PAIR), 1)
+    wkv = jnp.concatenate([wk_ref[...], wv_ref[...]], axis=1)
+
+    def finish(i, carry):
+        rows = pl.ds(pl.multiple_of(i * BLOCK, BLOCK), BLOCK)
+        g = dka[rows, :]
+        dk = (g * cos_ref[rows, :] - swap_halves(g, lane) * sin_ref[rows, :]).astype(jnp.bfloat16)
+        block = jnp.concatenate([dk, dva[rows, :].astype(jnp.bfloat16)], axis=1)
+        dkv[rows, :] = block
+        grown = contract(block, wkv, 1, 1)
+
+        @pl.when(p == 0)
+        def _():
+            acc[rows, :] = grown
+
+        @pl.when(p > 0)
+        def _():
+            acc[rows, :] += grown
+
+        return carry
+
+    lax.fori_loop(0, total // BLOCK, finish, 0)
+
+    def finish_query(i, carry):
+        rows = pl.ds(pl.multiple_of(i * BLOCK, BLOCK), BLOCK)
+        here = pl.ds(pl.multiple_of(i * BLOCK + W, BLOCK), BLOCK)
+        acc[here, :] += contract(dqs[rows, :], wq_ref[...], 1, 1)
+        return carry
+
+    lax.fori_loop(0, own // BLOCK, finish_query, 0)
+
+    def x_copy(j):
+        return remote(xs.at[j], xr.at[j], x_send.at[j], x_recv.at[j], partner)
+
+    def own_copy():
+        return remote(
+            ys, yr, x_send.at[chunks], x_recv.at[chunks], partner
+        )
+
+    @pl.when(p == last)
+    def _():
+        for j in range(chunks):
+            xs[j] = acc[pl.ds(other_at + j * piece, piece), :].astype(jnp.bfloat16)
+            x_copy(j).start()
+        ys[...] = acc[pl.ds(W + other_at, half), :].astype(jnp.bfloat16)
+        own_copy().start()
+
+    def project_grad(j, carry):
+        cols = pl.ds(pl.multiple_of(j * BLOCK, BLOCK), BLOCK)
+        part[p, cols, :PAIR] = contract(nx_ref[W:, cols], dqs[...], 0, 0).astype(jnp.bfloat16)
+        part[p, cols, PAIR:] = contract(nx_ref[:, cols], dkv[...], 0, 0).astype(jnp.bfloat16)
+        return carry
+
+    lax.fori_loop(0, D // BLOCK, project_grad, 0)
+
+    def fwd_copy(j):
+        return remote(fwd.at[j], later.at[j], fwd_send.at[j], fwd_recv.at[j], lax.rem(me + count - 2, count))
+
+    @pl.when(p == last)
+    def _():
+        for j in range(chunks):
+            x_copy(j).wait_recv()
+            mine = acc[pl.ds(mine_at + j * piece, piece), :]
+            fwd[j] = (mine + xr[j].astype(jnp.float32)).astype(jnp.bfloat16)
+
+            @pl.when(me >= 2)
+            def _():
+                fwd_copy(j).start()
+
+    def part_copy(pair, i):
+        target = lax.rem(me + 1 + i, count)
+        return remote(
+            part.at[pair, pl.ds(pl.multiple_of(target * share, share), share), :],
+            sums.at[pair, i], part_send.at[pair, i], part_recv.at[pair, i], target,
+        )
+
+    def send_part(i, carry):
+        part_copy(p, i).start()
+        return carry
+
+    lax.fori_loop(0, count - 1, send_part, 0)
+
+    @pl.when(p == last)
+    def _():
+        for pair in range(3):
+            ctx_copy(pair).wait()
+            mine_cols = pl.ds(pl.multiple_of(core * HALF + pair * PAIR, PAIR), PAIR)
+            other_cols = pl.ds(pl.multiple_of((1 - core) * HALF + pair * PAIR, PAIR), PAIR)
+            ctx_ref[:, mine_cols] = ctxs[pair, pl.ds(mine_at, half), :]
+            ctx_ref[:, other_cols] = ctxr[pair]
+
+        def sum_pair(pair):
+            def arrive(i, carry):
+                part_copy(pair, i).wait()
+                return carry
+
+            lax.fori_loop(0, count - 1, arrive, 0)
+
+            def add(i, carry):
+                odd, even = carry
+                return (
+                    odd + sums[pair, 2 * i].astype(jnp.float32),
+                    even + sums[pair, 2 * i + 1].astype(jnp.float32),
+                )
+
+            kept = part[pair, pl.ds(pl.multiple_of(me * share, share), share), :]
+            odd, even = lax.fori_loop(
+                0, count // 2 - 1, add,
+                (jnp.zeros((share, 3 * PAIR), jnp.float32), kept.astype(jnp.float32)),
+            )
+            odd = odd + sums[pair, count - 2].astype(jnp.float32)
+            for t in range(3):
+                at = t * D + pair * PAIR
+                a = pl.ds(pl.multiple_of(at + core * HALF, PAIR), PAIR)
+                b = pl.ds(pl.multiple_of(at + (1 - core) * HALF, PAIR), PAIR)
+                pg_ref[:, a] = even[:, t * PAIR : (t + 1) * PAIR] * grad_scale
+                pg_ref[:, b] = odd[:, t * PAIR : (t + 1) * PAIR] * grad_scale
+
+        sum_pair(0)
+        sum_pair(1)
+        own_copy().wait()
+        for j in range(chunks):
+            x_copy(j).wait_send()
+        ng_ref[...] = acc[pl.ds(W + mine_at, half), :] + yr[...].astype(jnp.float32)
+        sum_pair(2)
+        for j in range(chunks):
+
+            @pl.when(me >= 2)
+            def _():
+                fwd_copy(j).wait_send()
+
+            @pl.when(me < count - 2)
+            def _():
+                fwd_copy(j).wait_recv()
+                ng_ref[j * piece : (j + 1) * piece, :] += later[j].astype(jnp.float32)
+
+
+def fused(count, grad_scale, nx, weights, cosine, sine, seg_q, seg_k, out_grads):
+    total = nx.shape[0]
+    own = total - W
+    half = own // 2
+    pairs = HALF // PAIR
+    share = D // count
+    chunks = 4
+    whole = pl.BlockSpec(memory_space=pltpu.VMEM)
+
+    def columns(start):
+        return pl.BlockSpec((D, PAIR), lambda p: (0, start + p))
+
+    bf16, f32 = jnp.bfloat16, jnp.float32
+    return pl.pallas_call(
+        functools.partial(fused_kernel, count=count, grad_scale=grad_scale),
+        out_shape=[
+            jax.ShapeDtypeStruct((half, D), bf16),
+            jax.ShapeDtypeStruct((half, D), f32),
+            jax.ShapeDtypeStruct((share, 3 * D), f32),
+        ],
+        grid=(pairs,),
+        in_specs=[
+            whole, columns(0), columns(pairs), columns(2 * pairs), whole, whole, whole, whole,
+            pl.BlockSpec((own, PAIR), lambda p: (0, p)),
+        ],
+        out_specs=[whole, whole, whole],
+        scratch_shapes=[
+            pltpu.VMEM((own // BLOCK, BLOCK, SPAN), f32),
+            pltpu.VMEM((own, PAIR), bf16),
+            pltpu.VMEM((total, PAIR), bf16),
+            pltpu.VMEM((total, PAIR), bf16),
+            pltpu.VMEM((total, PAIR), f32),
+            pltpu.VMEM((total, PAIR), f32),
+            pltpu.VMEM((own, PAIR), bf16),
+            pltpu.VMEM((total, 2 * PAIR), bf16),
+            pltpu.VMEM((pairs, own, PAIR), bf16),
+            pltpu.VMEM((pairs, half, PAIR), bf16),
+            pltpu.VMEM((total, D), f32),
+            pltpu.VMEM((pairs, D, 3 * PAIR), bf16),
+            pltpu.VMEM((pairs, count - 1, share, 3 * PAIR), bf16),
+            pltpu.VMEM((chunks, half // chunks, D), bf16),
+            pltpu.VMEM((chunks, half // chunks, D), bf16),
+            pltpu.VMEM((half, D), bf16),
+            pltpu.VMEM((half, D), bf16),
+            pltpu.VMEM((chunks, half // chunks, D), bf16),
+            pltpu.VMEM((chunks, half // chunks, D), bf16),
+            pltpu.SemaphoreType.DMA((pairs, count - 1)),
+            pltpu.SemaphoreType.DMA((pairs, count - 1)),
+            pltpu.SemaphoreType.DMA((pairs,)),
+            pltpu.SemaphoreType.DMA((pairs,)),
+            pltpu.SemaphoreType.DMA((chunks + 1,)),
+            pltpu.SemaphoreType.DMA((chunks + 1,)),
+            pltpu.SemaphoreType.DMA((chunks,)),
+            pltpu.SemaphoreType.DMA((chunks,)),
+        ],
+        compiler_params=pltpu.CompilerParams(
+            vmem_limit_bytes=56 * 1024 * 1024, collective_id=0, has_side_effects=True
+        ),
+        name="fused_attention",
+    )(nx, weights, weights, weights, cosine, sine, seg_q, seg_k, out_grads)
+
+
+def own_columns(weights, core):
+    return jnp.concatenate(
+        [lax.dynamic_slice_in_dim(weights, t * D + core * HALF, HALF, 1) for t in range(3)], axis=1
+    )
+
+
 def swapped(value):
     count = lax.axis_size("seq")
     return lax.ppermute(value, "seq", [(s, s ^ 1) for s in range(count)])
@@ -224,6 +504,20 @@
     outside = (jnp.arange(seg_all.shape[0]) < W) & (chip == 0)
     seg_k = jnp.where(outside, -1, seg_all)[None, :]
     seg_q = seg_all[W:][:, None]
+
+    x_float = inputs.astype(jnp.float32)
+    inv_rms = lax.rsqrt(jnp.mean(x_float * x_float, axis=1, keepdims=True) + EPSILON)
+    scaled = x_float * inv_rms
+
+    if (D // device_count) % 16 == 0:
+        context, normed_grad, projection_grad = fused(
+            device_count, grad_scale, nx, own_columns(weights, core), cosine, sine, seg_q, seg_k,
+            out_grads,
+        )
+        input_grad = (
+            inv_rms * (normed_grad - scaled * jnp.mean(normed_grad * scaled, axis=1, keepdims=True))
+        ).astype(jnp.bfloat16)
+        return (context, input_grad, projection_grad)
 
     context_heads, dq, dk, dv = attention(
         core.astype(jnp.int32)[None], nx, weights, cosine, sine, seg_q, seg_k, out_grads
@@ -253,9 +547,6 @@
     normed_grad = (
         keep_own + swapped(send_own).astype(jnp.float32) + later.astype(jnp.float32)
     )
-    x_float = inputs.astype(jnp.float32)
-    inv_rms = lax.rsqrt(jnp.mean(x_float * x_float, axis=1, keepdims=True) + EPSILON)
-    scaled = x_float * inv_rms
     input_grad = (
         inv_rms * (normed_grad - scaled * jnp.mean(normed_grad * scaled, axis=1, keepdims=True))
     ).astype(jnp.bfloat16)

time: 225 us -> 187 us (0.83)
  Pallas kernels: 57.9 us -> 111 us
  waiting for transfers between devices: 78.9 us -> 26.4 us
  local copies, waits for them, and re-layouts: 22.4 us -> 5.34 us
  matrix products: 9.36 us -> 0 us
  starting transfers between devices: 15.4 us -> 9.15 us
  other arithmetic: 25 us -> 21.3 us
    pallas_call x1, Pallas kernels: 57.9 us -> 111 us  [fused(): pl.pallas_call(functools.partial(fused_kernel, count=count, grad_scale=gr...]
    unnamed x3 -> x1, waiting for transfers between devices: 29.5 us -> 0.68 us
    ppermute x3 -> x2, waiting for transfers between devices: 37.7 us -> 14.7 us  [chip_shifted(): return lax.ppermute(value, 'seq', pairs)]
    unnamed x48 -> x12, local copies, waits for them, and re-layouts: 16.2 us -> 1.66 us
    dot_general x4 -> x0, matrix products: 9.36 us -> none  [contract(): lax.dot_general(a, b, (((da,), (db,)), ((), ())), preferred_element_type=...]
    ppermute x3 -> x2, starting transfers between devices: 9.4 us -> 6.27 us  [chip_shifted(): return lax.ppermute(value, 'seq', pairs)]
    ppermute x9 -> x5, starting transfers between devices: 5.93 us -> 2.84 us  [swapped(): return lax.ppermute(value, 'seq', [(s, s ^ 1) for s in range(count)])]
    select_n x6 -> x5, other arithmetic: 3.72 us -> 1.12 us  [ordered(): first = jnp.where(core == 0, mine, other)]
  transfers between devices with their start and end apart: 14 -> 8, of which waited for: 6 -> 2; matrix products, arithmetic and copies ran while one was open for 16% -> 10% of each run, Pallas kernels for 0% -> 0%
where the time goes in v2:
time: 187 us
  Pallas kernels  111 us (59%)
  waiting for transfers between devices  26.4 us (14%)
  other arithmetic  21.3 us (11%)
  between operations  14.2 us (8%)
  starting transfers between devices  9.15 us (5%)
  local copies, waits for them, and re-layouts  5.34 us (3%)
    pallas_call x1, Pallas kernels, fused(): pl.pallas_call(functools.partial(fused_kernel, count=count, grad_scale=gr...  111 us
    ppermute x2, waiting for transfers between devices, chip_shifted(): return lax.ppermute(value, 'seq', pairs)  14.7 us
    all_gather x1, waiting for transfers between devices, local(): weights = lax.all_gather(projection, 'seq', axis=0, tiled=True)  10.9 us
    ppermute x2, starting transfers between devices, chip_shifted(): return lax.ppermute(value, 'seq', pairs)  6.27 us
    convert_element_type x1, other arithmetic, local(): nx = (x_all * lax.rsqrt(jnp.mean(x_all * x_all, axis=1, keepdims=True) +...  4.13 us
  transfers between devices with their start and end apart: 8, of which 2 were waited for; matrix products, arithmetic and copies ran while one was open for 10% of the time, Pallas kernels for 0%

profile of v2, /device:TPU:11, one launch (start us, length us, event | category | flops | bytes accessed | tf_op | source)
XLA Modules:
  0.0 187.1 jit_solution(16561845962478481489)
XLA Ops:
  7.2 0.0 all-gather.2.cloned.1.call-start
  7.2 0.7 all-gather.2.cloned.1.call-update
  7.9 0.7 pad_add_fusion.2
  8.6 3.2 %collective-permute-start.3 = (s32[2,512]{1,0:T(2,128)S(1)}, s32[2,512]{1,0:T(2,128)S(1)}, u32[]{:S(2)}, u32[]{:S(2)}) collective-permute-start(s32[2,512]{1,0:T(2,128)S(1)} %pad_add_fusion.2), channel_id=1, source_target_pairs={{0,2},{1,3},{2,4},{3,5},{4,6},{5,7},{6,8},{7,9},{8,10},{9,11},{10,... | collective-permute-start | bytes 12296 | tf_op jit(solution)/shard_map/ppermute | solution.py:454
  11.8 1.0 collective-permute-start.5
  12.8 3.1 %collective-permute-start = (bf16[512,768]{1,0:T(8,128)(2,1)}, bf16[512,768]{1,0:T(8,128)(2,1)S(1)}, u32[]{:S(2)}, u32[]{:S(2)}) collective-permute-start(bf16[512,768]{1,0:T(8,128)(2,1)} %param.5), channel_id=1, source_target_pairs={{0,2},{1,3},{2,4},{3,5},{4,6},{5,7},{6,8},{7,9},{8,10},{9,11},{10,... | collective-permute-start | bytes 2359304 | tf_op jit(solution)/shard_map/ppermute | solution.py:454
  15.9 0.4 collective-permute-start.2
  16.3 1.0 constant_dynamic-slice_fusion
  17.3 0.3 collective-permute-start.6
  17.6 1.4 fusion.8
  19.0 0.0 collective-permute-done.3
  19.0 0.4 collective-permute-start.4
  19.4 0.0 collective-permute-done.5
  19.4 0.7 broadcast_select_fusion.7
  20.1 1.0 copy.10.segq_ref
  21.2 0.0 collective-permute-done.4
  21.2 0.6 and_select_fusion
  21.8 3.7 %fusion.9 = (f32[2048,32]{1,0:T(8,128)S(1)}, f32[2048,32]{1,0:T(8,128)S(1)}, f32[2048,32]{1,0:T(8,128)S(1)}) fusion(f32[32]{0:T(128)S(1)} %multiply_exponential_fusion, f32[2048]{0:T(1024)S(1)} %bitcast.5), kind=kLoop, calls=%fused_computation.26 | loop fusion | flops 131072 | bytes 794752 | tf_op jit(solution)/shard_map/neg | solution.py:502
  25.5 0.0 copy-start.3
  25.5 14.7 %collective-permute-done = bf16[512,768]{1,0:T(8,128)(2,1)S(1)} collective-permute-done((bf16[512,768]{1,0:T(8,128)(2,1)}, bf16[512,768]{1,0:T(8,128)(2,1)S(1)}, u32[]{:S(2)}, u32[]{:S(2)}) %collective-permute-start) | collective-permute-done | bytes 786464 | tf_op jit(solution)/shard_map/ppermute | solution.py:454
  40.3 0.8 collective-permute-start.1
  41.1 0.0 copy-start
  41.1 3.0 %pad_maximum_fusion.2 = (f32[2048,128]{1,0:T(8,128)}, f32[2048,128]{1,0:T(8,128)}) fusion(f32[2048,32]{1,0:T(8,128)S(1)} %get-tuple-element.22, f32[2048,32]{1,0:T(8,128)S(1)} %get-tuple-element.21, f32[2048,32]{1,0:T(8,128)S(1)} %get-tuple-element.20), kind=kLoop, calls=%fused_computation.17 | loop fusion | flops 1572864 | bytes 2883584 | tf_op jit(solution)/shard_map/concatenate | solution.py:501
  44.1 0.0 collective-permute-done.6
  44.1 0.0 copy-done.3
  44.1 0.2 broadcast_select_fusion.5
  44.3 1.0 pad_maximum_fusion.4.do_ref
  45.3 0.0 collective-permute-done.2
  45.3 0.0 copy-done
  45.3 0.1 broadcast_select_fusion.1
  45.4 0.0 collective-permute-done.1
  45.4 0.1 broadcast_select_fusion.3
  45.5 1.0 fusion
  46.5 4.1 %fusion.1.nx_ref = bf16[2048,768]{1,0:T(8,128)(2,1)} fusion(f32[2048]{0:T(1024)S(1)} %add_rsqrt_fusion, bf16[512,768]{1,0:T(8,128)(2,1)S(1)} %get-tuple-element.15, bf16[512,768]{1,0:T(8,128)(2,1)S(1)} %get-tuple-element.14, bf16[512,768]{1,0:T(8,128)(2,1)S(1)} %get-tuple-element.13, bf16[512,768]{1,0:T(8,128)(2,1)S(1)} %get-tuple-element.12), kind=kLoop, calls=%fused_computation.3 | loop fusion | flops 15728640 | bytes 6299648 | tf_op jit(solution)/shard_map/convert_element_type | solution.py:492
  50.7 10.9 %all-gather.2.cloned.1.call-done = bf16[768,2304]{1,0:T(8,128)(2,1)} async-done(((bf16[48,2304]{1,0:T(8,128)(2,1)}), bf16[768,2304]{1,0:T(8,128)(2,1)}) %all-gather.2.cloned.1.call-update) | async-done | bytes 3538960 | tf_op jit(solution)/shard_map/all_gather | solution.py:473
  61.6 1.6 constant_dynamic-slice_fusion.3
  63.2 1.4 pad_maximum_fusion.1.wq_ref.wk_ref.wv_ref
  64.6 110.8 %fused_attention.1 = (bf16[512,768]{1,0:T(8,128)(2,1)}, f32[512,768]{1,0:T(8,128)}, f32[48,2304]{1,0:T(8,128)}) custom-call(bf16[2048,768]{1,0:T(8,128)(2,1)} %fusion.1.nx_ref, bf16[768,1152]{1,0:T(8,128)(2,1)} %pad_maximum_fusion.1.wq_ref.wk_ref.wv_ref, bf16[768,1152]{1,0:T(8,128)(2,1)} %pad_maximum_fusion.1.wq_ref.wk_ref.wv_ref, ...), custom_call_target="tpu_custom_call" | custom-call | tf_op jit(solution)/shard_map/fused_attention/pallas_call | solution.py:391
  175.4 0.0 copy-start.1
  175.4 0.0 copy-start.2
  175.4 0.0 copy-start.4
  175.4 1.9 %fusion.4 = f32[512]{0:T(512)S(1)} fusion(f32[512,768]{1,0:T(8,128)} %get-tuple-element.7, bf16[512,768]{1,0:T(8,128)(2,1)S(1)} %copy-done, f32[512]{0:T(512)S(1)} %add_rsqrt_fusion.1), kind=kLoop, calls=%fused_computation.10 | loop fusion | flops 1572352 | bytes 2363392 | tf_op jit(solution)/shard_map/reduce_sum | solution.py:518
  177.4 0.0 copy-done.1
  177.4 1.2 fusion.7
  178.6 0.0 copy-done.2
  178.6 0.9 copy.13
  179.5 0.0 copy-done.4
  179.5 0.8 copy.14
  (7 shorter events, 0.0 us)
Async XLA Ops:
  7.2 54.4 %all-gather.2.cloned.1.call-start = ((), (), s32[]{:S(2)}) async-start(), calls=%async_computation | async-start | bytes 3760128 | tf_op jit(solution)/shard_map/all_gather | solution.py:473
  8.6 10.4 %collective-permute-start.3 = (s32[2,512]{1,0:T(2,128)S(1)}, s32[2,512]{1,0:T(2,128)S(1)}, u32[]{:S(2)}, u32[]{:S(2)}) collective-permute-start(s32[2,512]{1,0:T(2,128)S(1)} %pad_add_fusion.2), channel_id=1, source_target_pairs={{0,2},{1,3},{2,4},{3,5},{4,6},{5,7},{6,8},{7,9},{8,10},{9,11},{10,... | collective-permute-start | bytes 12296 | tf_op jit(solution)/shard_map/ppermute | solution.py:454
  11.8 7.6 %collective-permute-start.5 = (s32[2,512]{1,0:T(2,128)S(1)}, s32[2,512]{1,0:T(2,128)S(1)}, u32[]{:S(2)}, u32[]{:S(2)}) collective-permute-start(s32[2,512]{1,0:T(2,128)S(1)} %pad_add_fusion.2), channel_id=1, source_target_pairs={{0,1},{1,0},{2,3},{3,2},{4,5},{5,4},{6,7},{7,6},{8,9},{9,8},{10,11... | collective-permute-start | bytes 12296 | tf_op jit(solution)/shard_map/ppermute | solution.py:448
  12.8 27.5 %collective-permute-start = (bf16[512,768]{1,0:T(8,128)(2,1)}, bf16[512,768]{1,0:T(8,128)(2,1)S(1)}, u32[]{:S(2)}, u32[]{:S(2)}) collective-permute-start(bf16[512,768]{1,0:T(8,128)(2,1)} %param.5), channel_id=1, source_target_pairs={{0,2},{1,3},{2,4},{3,5},{4,6},{5,7},{6,8},{7,9},{8,10},{9,11},{10,... | collective-permute-start | bytes 2359304 | tf_op jit(solution)/shard_map/ppermute | solution.py:454
  15.9 29.4 %collective-permute-start.2 = (bf16[512,768]{1,0:T(8,128)(2,1)}, bf16[512,768]{1,0:T(8,128)(2,1)S(1)}, u32[]{:S(2)}, u32[]{:S(2)}) collective-permute-start(bf16[512,768]{1,0:T(8,128)(2,1)} %param.5), channel_id=1, source_target_pairs={{0,1},{1,0},{2,3},{3,2},{4,5},{5,4},{6,7},{7,6},{8,9},{9,8},{10,11... | collective-permute-start | bytes 2359304 | tf_op jit(solution)/shard_map/ppermute | solution.py:448
  17.3 26.8 %collective-permute-start.6 = (bf16[512,384]{1,0:T(8,128)(2,1)S(1)}, bf16[512,384]{1,0:T(8,128)(2,1)S(1)}, u32[]{:S(2)}, u32[]{:S(2)}) collective-permute-start(bf16[512,384]{1,0:T(8,128)(2,1)S(1)} %constant_dynamic-slice_fusion), channel_id=1, source_target_pairs={{0,1},{1,0},{2,3},{3,2},{4,5},{5,4},{6,7},{7,6},{8,9},{9,8},{10,11... | collective-permute-start | bytes 1179656 | tf_op jit(solution)/shard_map/ppermute | solution.py:448
  19.0 2.1 %collective-permute-start.4 = (s32[2,512]{1,0:T(2,128)S(1)}, s32[2,512]{1,0:T(2,128)S(1)}, u32[]{:S(2)}, u32[]{:S(2)}) collective-permute-start(s32[2,512]{1,0:T(2,128)S(1)} %collective-permute-done.3), channel_id=1, source_target_pairs={{0,1},{1,0},{2,3},{3,2},{4,5},{5,4},{6,7},{7,6},{8,9},{9,8},{10,11... | collective-permute-start | bytes 12296 | tf_op jit(solution)/shard_map/ppermute | solution.py:448
  25.5 18.6 %copy-start.3 = (bf16[512,768]{1,0:T(8,128)(2,1)S(1)}, bf16[512,768]{1,0:T(8,128)(2,1)}, u32[]{:S(2)}) copy-start(bf16[512,768]{1,0:T(8,128)(2,1)} %param.9) | copy-start | bytes 2359300
  40.3 5.1 %collective-permute-start.1 = (bf16[512,768]{1,0:T(8,128)(2,1)S(1)}, bf16[512,768]{1,0:T(8,128)(2,1)S(1)}, u32[]{:S(2)}, u32[]{:S(2)}) collective-permute-start(bf16[512,768]{1,0:T(8,128)(2,1)S(1)} %collective-permute-done), channel_id=1, source_target_pairs={{0,1},{1,0},{2,3},{3,2},{4,5},{5,4},{6,7},{7,6},{8,9},{9,8},{10,11... | collective-permute-start | bytes 2359304 | tf_op jit(solution)/shard_map/ppermute | solution.py:448
  41.1 4.2 %copy-start = (bf16[512,768]{1,0:T(8,128)(2,1)S(1)}, bf16[512,768]{1,0:T(8,128)(2,1)}, u32[]{:S(2)}) copy-start(bf16[512,768]{1,0:T(8,128)(2,1)} %param.5) | copy-start | bytes 2359300
  175.4 2.0 %copy-start.1 = (f32[512,768]{1,0:T(8,128)S(1)}, f32[512,768]{1,0:T(8,128)}, u32[]{:S(2)}) copy-start(f32[512,768]{1,0:T(8,128)} %get-tuple-element.7) | copy-start | bytes 4718596
  175.4 3.2 %copy-start.2 = (bf16[512,768]{1,0:T(8,128)(2,1)S(1)}, bf16[512,768]{1,0:T(8,128)(2,1)}, u32[]{:S(2)}) copy-start(bf16[512,768]{1,0:T(8,128)(2,1)} %get-tuple-element.32) | copy-start | bytes 2359300
  175.4 4.1 %copy-start.4 = (f32[48,2304]{1,0:T(8,128)S(1)}, f32[48,2304]{1,0:T(8,128)}, u32[]{:S(2)}) copy-start(f32[48,2304]{1,0:T(8,128)} %get-tuple-element.34) | copy-start | bytes 1327108
Sparse Core Ops, SparseCore 0:
  10.3 51.2 all-gather.1

commit v3 on v2

--- a/solution.py
+++ b/solution.py
@@ -30,8 +30,17 @@
     return jnp.where(low, pltpu.roll(u, PAIR - HD // 2, 1), pltpu.roll(u, HD // 2, 1))
 
 
+def fill_bias(bias, segq_ref, segk_ref):
+    row = lax.broadcasted_iota(jnp.int32, (BLOCK, SPAN), 0)
+    col = lax.broadcasted_iota(jnp.int32, (BLOCK, SPAN), 1)
+    near = (col > row) & (col <= row + W)
+    for b in range(bias.shape[0]):
+        same = segq_ref[b * BLOCK : (b + 1) * BLOCK, :] == segk_ref[:, b * BLOCK : b * BLOCK + SPAN]
+        bias[b] = jnp.where(near & same, 0.0, MASKED_SCORE)
+
+
 def pair_attention(
-    p, nx_ref, wq_ref, wk_ref, wv_ref, cos_ref, sin_ref, segq_ref, segk_ref, do_ref,
+    nx_ref, wq_ref, wk_ref, wv_ref, cos_ref, sin_ref, do_ref,
     ctx_ref, dq_ref,
     bias, qs, ks, vs, dka, dva,
 ):
@@ -41,15 +50,6 @@
 
     def swap(u):
         return swap_halves(u, lane)
-
-    @pl.when(p == 0)
-    def _():
-        row = lax.broadcasted_iota(jnp.int32, (BLOCK, SPAN), 0)
-        col = lax.broadcasted_iota(jnp.int32, (BLOCK, SPAN), 1)
-        near = (col > row) & (col <= row + W)
-        for b in range(own // BLOCK):
-            same = segq_ref[b * BLOCK : (b + 1) * BLOCK, :] == segk_ref[:, b * BLOCK : b * BLOCK + SPAN]
-            bias[b] = jnp.where(near & same, 0.0, MASKED_SCORE)
 
     def project(i, carry):
         rows = pl.ds(pl.multiple_of(i * BLOCK, BLOCK), BLOCK)
@@ -77,7 +77,7 @@
         rows = pl.ds(pl.multiple_of(b * BLOCK, BLOCK), BLOCK)
         here = pl.ds(pl.multiple_of(b * BLOCK + W, BLOCK), BLOCK)
         window = pl.ds(pl.multiple_of(b * BLOCK, BLOCK), SPAN)
-        contexts, grads = [], []
+        contexts, grads, keep = [], [], []
         for h in range(2):
             mine = (lane // HD) == h
             kb = ks[window, :]
@@ -96,15 +96,19 @@
             ds = (w * (dp - delta)).astype(jnp.bfloat16)
             contexts.append(context)
             grads.append(contract(ds, kb, 1, 0))
-            dka[window, :] += contract(ds, qh, 0, 0)
-            dva[window, :] += contract(pb, gh, 0, 0)
+            keep.append((ds, qh, pb, gh))
+        ds, qh, pb, gh = [
+            jnp.concatenate([keep[0][n], keep[1][n]], axis=0) for n in range(4)
+        ]
+        dka[window, :] += contract(qh, ds, 0, 0).T
+        dva[window, :] += contract(gh, pb, 0, 0).T
         first = lane < HD
         ctx_ref[rows, :] = jnp.where(first, contexts[0], contexts[1])
         g = jnp.where(first, grads[0], grads[1]) * SCORE_SCALE
         dq_ref[rows, :] = (g * cos_ref[here, :] - swap(g) * sin_ref[here, :]).astype(jnp.bfloat16)
         return carry
 
-    lax.fori_loop(0, own // BLOCK, visit, 0)
+    lax.fori_loop(0, own // BLOCK, visit, 0, unroll=2)
 
 
 def attention_kernel(
@@ -118,9 +122,12 @@
     def swap(u):
         return swap_halves(u, lane)
 
+    @pl.when(pl.program_id(0) == 0)
+    def _():
+        fill_bias(bias, segq_ref, segk_ref)
+
     pair_attention(
-        pl.program_id(0), nx_ref, wq_ref, wk_ref, wv_ref, cos_ref, sin_ref, segq_ref, segk_ref,
-        do_ref, ctx_ref, dq_ref, bias, qs, ks, vs, dka, dva,
+        nx_ref, wq_ref, wk_ref, wv_ref, cos_ref, sin_ref, do_ref, ctx_ref, dq_ref, bias, qs, ks, vs, dka, dva,
     )
 
     def finish(i, carry):
@@ -185,8 +192,9 @@
 
 
 def fused_kernel(
-    nx_ref, wq_ref, wk_ref, wv_ref, cos_ref, sin_ref, segq_ref, segk_ref, do_ref,
+    own_ref, wl_ref, cos_ref, sin_ref, segq_ref, segk_ref, cg_ref,
     ctx_ref, ng_ref, pg_ref,
+    nx_ref, wbuf, gbuf, w_send, w_recv, n_send, n_recv, g_send, g_recv,
     bias, qs, ks, vs, dka, dva, dqs, dkv, ctxs, ctxr, acc, part, sums, xs, xr, ys, yr, fwd, later,
     part_send, part_recv, ctx_send, ctx_recv, x_send, x_recv, fwd_send, fwd_recv,
     *, count, grad_scale,
@@ -202,6 +210,10 @@
     share = D // count
     chunks = xs.shape[0]
     piece = half // chunks
+    wq_ref = wbuf.at[p, :, :PAIR]
+    wk_ref = wbuf.at[p, :, PAIR : 2 * PAIR]
+    wv_ref = wbuf.at[p, :, 2 * PAIR :]
+    my_rows = pl.ds(pl.multiple_of(me * share, share), share)
     mine_at = pl.multiple_of(core * half, half)
     other_at = pl.multiple_of((1 - core) * half, half)
 
@@ -225,8 +237,92 @@
         lax.fori_loop(0, count - 1, greet, 0)
         pl.semaphore_wait(barrier, count - 1)
 
+    def w_copy(pair, i):
+        target = lax.rem(me + 1 + i, count)
+        return remote(
+            wl_ref.at[lax.rem(target, 2), pair], wbuf.at[pair, my_rows, :],
+            w_send.at[pair, i], w_recv.at[pair, i], target,
+        )
+
+    def send_weights(pair):
+        def start(i, carry):
+            w_copy(pair, i).start()
+            return carry
+
+        lax.fori_loop(0, count - 1, start, 0)
+
+    def g_copy(pair):
+        cols = pl.ds(pl.multiple_of((1 - core) * HALF + pair * PAIR, PAIR), PAIR)
+        return remote(
+            cg_ref.at[:, cols], gbuf.at[pair, pl.ds(mine_at, half), :],
+            g_send.at[pair], g_recv.at[pair], partner,
+        )
+
+    def partner_copy():
+        return remote(
+            own_ref, nx_ref.at[pl.ds(W + mine_at, half), :], n_send.at[0], n_recv.at[0], partner
+        )
+
+    def halo_copy():
+        return remote(
+            own_ref, nx_ref.at[pl.ds(mine_at, half), :], n_send.at[1], n_recv.at[1],
+            lax.rem(me + 2, count),
+        )
+
+    def relay_copy():
+        rows = pl.ds(mine_at, half)
+        return remote(nx_ref.at[rows, :], nx_ref.at[rows, :], n_send.at[2], n_recv.at[2], partner)
+
+    @pl.when(p == 0)
+    def _():
+        @pl.when(me < count - 2)
+        def _():
+            halo_copy().start()
+
+        send_weights(0)
+        partner_copy().start()
+        for pair in range(3):
+            g_copy(pair).start()
+        nx_ref[pl.ds(W + mine_at, half), :] = own_ref[...]
+        for pair in range(3):
+            wbuf[pair, my_rows, :] = wl_ref[core, pair]
+            cols = pl.ds(pl.multiple_of(core * HALF + pair * PAIR, PAIR), PAIR)
+            gbuf[pair, pl.ds(mine_at, half), :] = cg_ref[:, cols]
+
+        @pl.when(me < 2)
+        def _():
+            nx_ref[:W, :] = jnp.zeros((W, D), jnp.bfloat16)
+
+        fill_bias(bias, segq_ref, segk_ref)
+
+        @pl.when(me >= 2)
+        def _():
+            halo_copy().wait_recv()
+            relay_copy().start()
+
+    def arrive_weights(i, carry):
+        w_copy(p, i).wait()
+        return carry
+
+    lax.fori_loop(0, count - 1, arrive_weights, 0)
+    g_copy(p).wait()
+
+    @pl.when(p == 0)
+    def _():
+        send_weights(1)
+        send_weights(2)
+        partner_copy().wait()
+
+        @pl.when(me >= 2)
+        def _():
+            relay_copy().wait()
+
+        @pl.when(me < count - 2)
+        def _():
+            halo_copy().wait_send()
+
     pair_attention(
-        p, nx_ref, wq_ref, wk_ref, wv_ref, cos_ref, sin_ref, segq_ref, segk_ref, do_ref,
+        nx_ref, wq_ref, wk_ref, wv_ref, cos_ref, sin_ref, gbuf.at[p],
         ctxs.at[p], dqs, bias, qs, ks, vs, dka, dva,
     )
 
@@ -376,16 +472,13 @@
 
 
 def fused(count, grad_scale, nx, weights, cosine, sine, seg_q, seg_k, out_grads):
-    total = nx.shape[0]
-    own = total - W
-    half = own // 2
+    half = nx.shape[0]
+    own = 2 * half
+    total = own + W
     pairs = HALF // PAIR
     share = D // count
     chunks = 4
     whole = pl.BlockSpec(memory_space=pltpu.VMEM)
-
-    def columns(start):
-        return pl.BlockSpec((D, PAIR), lambda p: (0, start + p))
 
     bf16, f32 = jnp.bfloat16, jnp.float32
     return pl.pallas_call(
@@ -396,12 +489,18 @@
             jax.ShapeDtypeStruct((share, 3 * D), f32),
         ],
         grid=(pairs,),
-        in_specs=[
-            whole, columns(0), columns(pairs), columns(2 * pairs), whole, whole, whole, whole,
-            pl.BlockSpec((own, PAIR), lambda p: (0, p)),
-        ],
+        in_specs=[whole] * 7,
         out_specs=[whole, whole, whole],
         scratch_shapes=[
+            pltpu.VMEM((total, D), bf16),
+            pltpu.VMEM((pairs, D, 3 * PAIR), bf16),
+            pltpu.VMEM((pairs, own, PAIR), bf16),
+            pltpu.SemaphoreType.DMA((pairs, count - 1)),
+            pltpu.SemaphoreType.DMA((pairs, count - 1)),
+            pltpu.SemaphoreType.DMA((3,)),
+            pltpu.SemaphoreType.DMA((3,)),
+            pltpu.SemaphoreType.DMA((pairs,)),
+            pltpu.SemaphoreType.DMA((pairs,)),
             pltpu.VMEM((own // BLOCK, BLOCK, SPAN), f32),
             pltpu.VMEM((own, PAIR), bf16),
             pltpu.VMEM((total, PAIR), bf16),
@@ -434,13 +533,21 @@
             vmem_limit_bytes=56 * 1024 * 1024, collective_id=0, has_side_effects=True
         ),
         name="fused_attention",
-    )(nx, weights, weights, weights, cosine, sine, seg_q, seg_k, out_grads)
-
-
-def own_columns(weights, core):
-    return jnp.concatenate(
-        [lax.dynamic_slice_in_dim(weights, t * D + core * HALF, HALF, 1) for t in range(3)], axis=1
-    )
+    )(nx, weights, cosine, sine, seg_q, seg_k, out_grads)
+
+
+def tables(meta_all, chip):
+    half_size = HD // 2
+    frequency = jnp.exp(-math.log(10000.0) * jnp.arange(half_size, dtype=jnp.float32) / half_size)
+    angle = meta_all[0].astype(jnp.float32)[:, None] * frequency[None, :]
+    c, s = jnp.cos(angle), jnp.sin(angle)
+    cosine = jnp.concatenate([c, c, c, c], axis=1)
+    sine = jnp.concatenate([-s, s, -s, s], axis=1)
+    seg_all = meta_all[1]
+    outside = (jnp.arange(seg_all.shape[0]) < W) & (chip == 0)
+    seg_k = jnp.where(outside, -1, seg_all)[None, :]
+    seg_q = seg_all[W:][:, None]
+    return cosine, sine, seg_q, seg_k
 
 
 def swapped(value):
@@ -470,9 +577,33 @@
     assert 2 * row_count == W
     grad_scale = (row_count * device_count) ** (-0.5)
 
+    meta = jnp.stack([positions, segments], axis=0)
+    x_float = inputs.astype(jnp.float32)
+    inv_rms = lax.rsqrt(jnp.mean(x_float * x_float, axis=1, keepdims=True) + EPSILON)
+    scaled = x_float * inv_rms
+
+    if (D // device_count) % 16 == 0:
+        crossed = [(s, (s + 2) ^ 1) for s in range(device_count - 2)]
+        meta_all = jnp.concatenate(
+            [
+                ordered(core, chip_shifted(meta, 1), lax.ppermute(meta, "seq", crossed), 1),
+                ordered(core, meta, swapped(meta), 1),
+            ],
+            axis=1,
+        )
+        cosine, sine, seg_q, seg_k = tables(meta_all, chip)
+        pieces = projection.reshape(D // device_count, 3, 2, 3, PAIR)
+        pieces = jnp.transpose(pieces, (2, 3, 0, 1, 4)).reshape(2, 3, D // device_count, 3 * PAIR)
+        context, normed_grad, projection_grad = fused(
+            device_count, grad_scale, scaled.astype(jnp.bfloat16), pieces, cosine, sine, seg_q,
+            seg_k, context_grad,
+        )
+        input_grad = (
+            inv_rms * (normed_grad - scaled * jnp.mean(normed_grad * scaled, axis=1, keepdims=True))
+        ).astype(jnp.bfloat16)
+        return (context, input_grad, projection_grad)
+
     weights = lax.all_gather(projection, "seq", axis=0, tiled=True)
-
-    meta = jnp.stack([positions, segments], axis=0)
     x_before = chip_shifted(inputs, 1)
     meta_before = chip_shifted(meta, 1)
     x_other = swapped(inputs)
@@ -494,31 +625,7 @@
         [ordered(core, meta_before, meta_before_other, 1), ordered(core, meta, meta_other, 1)],
         axis=1,
     )
-    half_size = HD // 2
-    frequency = jnp.exp(-math.log(10000.0) * jnp.arange(half_size, dtype=jnp.float32) / half_size)
-    angle = meta_all[0].astype(jnp.float32)[:, None] * frequency[None, :]
-    c, s = jnp.cos(angle), jnp.sin(angle)
-    cosine = jnp.concatenate([c, c, c, c], axis=1)
-    sine = jnp.concatenate([-s, s, -s, s], axis=1)
-    seg_all = meta_all[1]
-    outside = (jnp.arange(seg_all.shape[0]) < W) & (chip == 0)
-    seg_k = jnp.where(outside, -1, seg_all)[None, :]
-    seg_q = seg_all[W:][:, None]
-
-    x_float = inputs.astype(jnp.float32)
-    inv_rms = lax.rsqrt(jnp.mean(x_float * x_float, axis=1, keepdims=True) + EPSILON)
-    scaled = x_float * inv_rms
-
-    if (D // device_count) % 16 == 0:
-        context, normed_grad, projection_grad = fused(
-            device_count, grad_scale, nx, own_columns(weights, core), cosine, sine, seg_q, seg_k,
-            out_grads,
-        )
-        input_grad = (
-            inv_rms * (normed_grad - scaled * jnp.mean(normed_grad * scaled, axis=1, keepdims=True))
-        ).astype(jnp.bfloat16)
-        return (context, input_grad, projection_grad)
-
+    cosine, sine, seg_q, seg_k = tables(meta_all, chip)
     context_heads, dq, dk, dv = attention(
         core.astype(jnp.int32)[None], nx, weights, cosine, sine, seg_q, seg_k, out_grads
     )

time: 187 us -> 161 us (0.86)
  waiting for transfers between devices: 26.4 us -> 0.01 us
  Pallas kernels: 111 us -> 134 us
  between operations: 14.2 us -> 0.79 us
  other arithmetic: 21.3 us -> 14.9 us
  starting transfers between devices: 9.15 us -> 7.2 us
    pallas_call x1, Pallas kernels: 111 us -> 134 us  [fused(): pl.pallas_call(functools.partial(fused_kernel, count=count, grad_scale=gr...]
    ppermute x2 -> x1, waiting for transfers between devices: 14.7 us -> 0.01 us  [chip_shifted(): return lax.ppermute(value, 'seq', pairs)]
    all_gather x1 -> x0, waiting for transfers between devices: 10.9 us -> none  [local(): weights = lax.all_gather(projection, 'seq', axis=0, tiled=True)]
    ppermute x0 -> x1, starting transfers between devices: none -> 3.96 us  [local(): lax.ppermute(meta, 'seq', crossed)]
    ppermute x2 -> x1, starting transfers between devices: 6.27 us -> 3.16 us  [chip_shifted(): return lax.ppermute(value, 'seq', pairs)]
    ppermute x5 -> x1, starting transfers between devices: 2.84 us -> 0.07 us  [swapped(): return lax.ppermute(value, 'seq', [(s, s ^ 1) for s in range(count)])]
    dynamic_slice x2 -> x0, local copies, waits for them, and re-layouts: 2.64 us -> none  [the longest x1 1.61 us: own_columns(): lax.dynamic_slice_in_dim(weights, t * D + core * HALF, HALF, 1)]
    concatenate x4 -> x2, other arithmetic: 5.43 us -> 3.02 us  [the longest x1 3.02 us: tables(): cosine = jnp.concatenate([c, c, c, c], axis=1)]
  transfers between devices with their start and end apart: 8 -> 3, of which waited for: 2 -> 0; matrix products, arithmetic and copies ran while one was open for 10% -> 4% of each run, Pallas kernels for 0% -> 0%
where the time goes in v3:
time: 161 us
  Pallas kernels  134 us (83%)
  other arithmetic  14.9 us (9%)
  starting transfers between devices  7.2 us (4%)
  local copies, waits for them, and re-layouts  4.21 us (3%)
    pallas_call x1, Pallas kernels, fused(): pl.pallas_call(functools.partial(fused_kernel, count=count, grad_scale=gr...  134 us
    ppermute x1, starting transfers between devices, local(): lax.ppermute(meta, 'seq', crossed)  3.96 us
    neg x1, other arithmetic, tables(): sine = jnp.concatenate([-s, s, -s, s], axis=1)  3.72 us
  transfers between devices with their start and end apart: 3, of which 0 were waited for; matrix products, arithmetic and copies ran while one was open for 4% of the time, Pallas kernels for 0%

profile of v3, /device:TPU:11, one launch (start us, length us, event | category | flops | bytes accessed | tf_op | source)
XLA Modules:
  0.0 161.1 jit_solution(3318529882368292183)
XLA Ops:
  0.6 0.0 copy-start.4
  0.6 0.7 pad_add_fusion.2
  1.4 3.2 %collective-permute-start = (s32[2,512]{1,0:T(2,128)S(1)}, s32[2,512]{1,0:T(2,128)S(1)}, u32[]{:S(2)}, u32[]{:S(2)}) collective-permute-start(s32[2,512]{1,0:T(2,128)S(1)} %pad_add_fusion.2), channel_id=1, source_target_pairs={{0,2},{1,3},{2,4},{3,5},{4,6},{5,7},{6,8},{7,9},{8,10},{9,11},{10,... | collective-permute-start | bytes 12296 | tf_op jit(solution)/shard_map/ppermute | solution.py:561
  4.6 4.0 %collective-permute-start.1 = (s32[2,512]{1,0:T(2,128)S(1)}, s32[2,512]{1,0:T(2,128)S(1)}, u32[]{:S(2)}, u32[]{:S(2)}) collective-permute-start(s32[2,512]{1,0:T(2,128)S(1)} %pad_add_fusion.2), channel_id=1, source_target_pairs={{0,3},{1,2},{2,5},{3,4},{4,7},{5,6},{6,9},{7,8},{8,11},{9,10},{10,... | collective-permute-start | bytes 12296 | tf_op jit(solution)/shard_map/ppermute | solution.py:589
  8.5 0.1 collective-permute-start.2
  8.6 1.4 fusion.7
  10.0 0.0 copy-start.5
  10.0 0.0 copy-start.6
  10.0 2.2 %fusion.2.own_ref = bf16[512,768]{1,0:T(8,128)(2,1)} fusion(bf16[512,768]{1,0:T(8,128)(2,1)} %param.5, f32[512]{0:T(512)S(1)} %add_rsqrt_fusion), kind=kLoop, calls=%fused_computation.4 | loop fusion | flops 1179648 | bytes 1574912 | tf_op jit(solution)/shard_map/convert_element_type | solution.py:598
  12.2 0.0 copy-done.4
  12.2 0.1 reshape.47
  12.3 0.1 copy.11
  12.5 0.9 reshape.48.wl_ref
  13.3 0.0 collective-permute-done.2
  13.4 0.0 copy-done.5
  13.4 0.0 copy-done.6
  13.4 1.0 copy.13.segq_ref
  14.4 0.0 collective-permute-done
  14.4 0.0 collective-permute-done.1
  14.5 0.6 and_select_fusion
  15.1 3.7 %fusion.8 = (f32[2048,32]{1,0:T(8,128)S(1)}, f32[2048,32]{1,0:T(8,128)S(1)}, f32[2048,32]{1,0:T(8,128)S(1)}) fusion(f32[32]{0:T(128)S(1)} %multiply_exponential_fusion, f32[2048]{0:T(1024)S(1)} %bitcast.7), kind=kLoop, calls=%fused_computation.14 | loop fusion | flops 131072 | bytes 794752 | tf_op jit(solution)/shard_map/neg | solution.py:545
  18.8 3.0 %pad_maximum_fusion = (f32[2048,128]{1,0:T(8,128)}, f32[2048,128]{1,0:T(8,128)}) fusion(f32[2048,32]{1,0:T(8,128)S(1)} %get-tuple-element.13, f32[2048,32]{1,0:T(8,128)S(1)} %get-tuple-element.12, f32[2048,32]{1,0:T(8,128)S(1)} %get-tuple-element.11), kind=kLoop, calls=%fused_computation.12 | loop fusion | flops 1572864 | bytes 2883584 | tf_op jit(solution)/shard_map/concatenate | solution.py:544
  21.8 0.0 copy-start
  21.8 134.0 %fused_attention.1 = (bf16[512,768]{1,0:T(8,128)(2,1)}, f32[512,768]{1,0:T(8,128)}, f32[48,2304]{1,0:T(8,128)}) custom-call(bf16[512,768]{1,0:T(8,128)(2,1)} %fusion.2.own_ref, bf16[2,3,48,384]{3,2,1,0:T(8,128)(2,1)} %reshape.48.wl_ref, f32[2048,128]{1,0:T(8,128)} %get-tuple-element.18.cos_ref, f32[2048,128]{1,0:T(8,128)} %get-tuple-element.19.sin_ref, ...), custom_call_target="tpu_custom_call" | custom-call | tf_op jit(solution)/shard_map/fused_attention/pallas_call | solution.py:484
  155.8 0.0 copy-start.1
  155.8 0.0 copy-done
  155.8 1.9 %fusion.3 = f32[512]{0:T(512)S(1)} fusion(f32[512,768]{1,0:T(8,128)} %get-tuple-element.7, bf16[512,768]{1,0:T(8,128)(2,1)S(1)} %copy-done, f32[512]{0:T(512)S(1)} %add_rsqrt_fusion), kind=kLoop, calls=%fused_computation.5 | loop fusion | flops 1572352 | bytes 2363392 | tf_op jit(solution)/shard_map/reduce_sum | solution.py:602
  157.7 0.0 copy-done.1
  157.8 0.0 copy-start.2
  157.8 1.2 fusion.6
  159.0 0.0 copy-start.3
  159.0 0.0 copy-done.2
  159.0 0.9 copy.16
  159.9 0.4 copy-done.3
  160.3 0.8 copy.17
  (7 shorter events, 0.1 us)
Async XLA Ops:
  0.6 11.6 %copy-start.4 = (bf16[48,2304]{1,0:T(8,128)(2,1)S(1)}, bf16[48,2304]{1,0:T(8,128)(2,1)}, u32[]{:S(2)}) copy-start(bf16[48,2304]{1,0:T(8,128)(2,1)} %param.6) | copy-start | bytes 663556
  1.4 13.0 %collective-permute-start = (s32[2,512]{1,0:T(2,128)S(1)}, s32[2,512]{1,0:T(2,128)S(1)}, u32[]{:S(2)}, u32[]{:S(2)}) collective-permute-start(s32[2,512]{1,0:T(2,128)S(1)} %pad_add_fusion.2), channel_id=1, source_target_pairs={{0,2},{1,3},{2,4},{3,5},{4,6},{5,7},{6,8},{7,9},{8,10},{9,11},{10,... | collective-permute-start | bytes 12296 | tf_op jit(solution)/shard_map/ppermute | solution.py:561
  4.6 9.9 %collective-permute-start.1 = (s32[2,512]{1,0:T(2,128)S(1)}, s32[2,512]{1,0:T(2,128)S(1)}, u32[]{:S(2)}, u32[]{:S(2)}) collective-permute-start(s32[2,512]{1,0:T(2,128)S(1)} %pad_add_fusion.2), channel_id=1, source_target_pairs={{0,3},{1,2},{2,5},{3,4},{4,7},{5,6},{6,9},{7,8},{8,11},{9,10},{10,... | collective-permute-start | bytes 12296 | tf_op jit(solution)/shard_map/ppermute | solution.py:589
  8.5 4.8 %collective-permute-start.2 = (s32[2,512]{1,0:T(2,128)S(1)}, s32[2,512]{1,0:T(2,128)S(1)}, u32[]{:S(2)}, u32[]{:S(2)}) collective-permute-start(s32[2,512]{1,0:T(2,128)S(1)} %pad_add_fusion.2), channel_id=1, source_target_pairs={{0,1},{1,0},{2,3},{3,2},{4,5},{5,4},{6,7},{7,6},{8,9},{9,8},{10,11... | collective-permute-start | bytes 12296 | tf_op jit(solution)/shard_map/ppermute | solution.py:555
  10.0 3.4 %copy-start.5 = (s32[512]{0:T(512)S(1)}, s32[512]{0:T(512)}, u32[]{:S(2)}) copy-start(s32[512]{0:T(512)} %param.8) | copy-start | bytes 6148
  10.0 3.4 %copy-start.6 = (s32[512]{0:T(512)S(1)}, s32[512]{0:T(512)}, u32[]{:S(2)}) copy-start(s32[512]{0:T(512)} %param.7) | copy-start | bytes 6148
  21.8 134.0 %copy-start = (bf16[512,768]{1,0:T(8,128)(2,1)S(1)}, bf16[512,768]{1,0:T(8,128)(2,1)}, u32[]{:S(2)}) copy-start(bf16[512,768]{1,0:T(8,128)(2,1)} %param.5) | copy-start | bytes 2359300
  155.8 1.9 %copy-start.1 = (f32[512,768]{1,0:T(8,128)S(1)}, f32[512,768]{1,0:T(8,128)}, u32[]{:S(2)}) copy-start(f32[512,768]{1,0:T(8,128)} %get-tuple-element.7) | copy-start | bytes 4718596
  157.8 1.2 copy-start.2
  159.0 1.3 copy-start.3

commit v4 on v3

--- a/solution.py
+++ b/solution.py
@@ -355,7 +355,23 @@
 
         return carry
 
-    lax.fori_loop(0, total // BLOCK, finish, 0)
+    lax.fori_loop(0, W // BLOCK, finish, 0)
+
+    def x_copy(j):
+        return remote(xs.at[j], xr.at[j], x_send.at[j], x_recv.at[j], partner)
+
+    def own_copy():
+        return remote(
+            ys, yr, x_send.at[chunks], x_recv.at[chunks], partner
+        )
+
+    @pl.when(p == last)
+    def _():
+        for j in range(chunks):
+            xs[j] = acc[pl.ds(other_at + j * piece, piece), :].astype(jnp.bfloat16)
+            x_copy(j).start()
+
+    lax.fori_loop(W // BLOCK, total // BLOCK, finish, 0)
 
     def finish_query(i, carry):
         rows = pl.ds(pl.multiple_of(i * BLOCK, BLOCK), BLOCK)
@@ -365,21 +381,24 @@
 
     lax.fori_loop(0, own // BLOCK, finish_query, 0)
 
-    def x_copy(j):
-        return remote(xs.at[j], xr.at[j], x_send.at[j], x_recv.at[j], partner)
-
-    def own_copy():
-        return remote(
-            ys, yr, x_send.at[chunks], x_recv.at[chunks], partner
-        )
-
     @pl.when(p == last)
     def _():
-        for j in range(chunks):
-            xs[j] = acc[pl.ds(other_at + j * piece, piece), :].astype(jnp.bfloat16)
-            x_copy(j).start()
         ys[...] = acc[pl.ds(W + other_at, half), :].astype(jnp.bfloat16)
         own_copy().start()
+
+    def fwd_copy(j):
+        return remote(fwd.at[j], later.at[j], fwd_send.at[j], fwd_recv.at[j], lax.rem(me + count - 2, count))
+
+    @pl.when(p == last)
+    def _():
+        for j in range(chunks):
+            x_copy(j).wait_recv()
+            mine = acc[pl.ds(mine_at + j * piece, piece), :]
+            fwd[j] = (mine + xr[j].astype(jnp.float32)).astype(jnp.bfloat16)
+
+            @pl.when(me >= 2)
+            def _():
+                fwd_copy(j).start()
 
     def project_grad(j, carry):
         cols = pl.ds(pl.multiple_of(j * BLOCK, BLOCK), BLOCK)
@@ -388,20 +407,6 @@
         return carry
 
     lax.fori_loop(0, D // BLOCK, project_grad, 0)
-
-    def fwd_copy(j):
-        return remote(fwd.at[j], later.at[j], fwd_send.at[j], fwd_recv.at[j], lax.rem(me + count - 2, count))
-
-    @pl.when(p == last)
-    def _():
-        for j in range(chunks):
-            x_copy(j).wait_recv()
-            mine = acc[pl.ds(mine_at + j * piece, piece), :]
-            fwd[j] = (mine + xr[j].astype(jnp.float32)).astype(jnp.bfloat16)
-
-            @pl.when(me >= 2)
-            def _():
-                fwd_copy(j).start()
 
     def part_copy(pair, i):
         target = lax.rem(me + 1 + i, count)

time: 161 us -> 160 us (level)
  no operation moved by 1% of the time
where the time goes in v4:
time: 160 us
  Pallas kernels  133 us (83%)
  other arithmetic  14.9 us (9%)
  starting transfers between devices  7.2 us (4%)
  local copies, waits for them, and re-layouts  4.21 us (3%)
    pallas_call x1, Pallas kernels, fused(): pl.pallas_call(functools.partial(fused_kernel, count=count, grad_scale=gr...  133 us
    ppermute x1, starting transfers between devices, local(): lax.ppermute(meta, 'seq', crossed)  3.96 us
    neg x1, other arithmetic, tables(): sine = jnp.concatenate([-s, s, -s, s], axis=1)  3.72 us
  transfers between devices with their start and end apart: 3, of which 0 were waited for; matrix products, arithmetic and copies ran while one was open for 4% of the time, Pallas kernels for 0%

profile of v4, /device:TPU:11, one launch (start us, length us, event | category | flops | bytes accessed | tf_op | source)
XLA Modules:
  0.0 159.9 jit_solution(14797159624892167926)
XLA Ops:
  0.6 0.0 copy-start.4
  0.6 0.7 pad_add_fusion.2
  1.4 3.2 %collective-permute-start = (s32[2,512]{1,0:T(2,128)S(1)}, s32[2,512]{1,0:T(2,128)S(1)}, u32[]{:S(2)}, u32[]{:S(2)}) collective-permute-start(s32[2,512]{1,0:T(2,128)S(1)} %pad_add_fusion.2), channel_id=1, source_target_pairs={{0,2},{1,3},{2,4},{3,5},{4,6},{5,7},{6,8},{7,9},{8,10},{9,11},{10,... | collective-permute-start | bytes 12296 | tf_op jit(solution)/shard_map/ppermute | solution.py:566
  4.6 4.0 %collective-permute-start.1 = (s32[2,512]{1,0:T(2,128)S(1)}, s32[2,512]{1,0:T(2,128)S(1)}, u32[]{:S(2)}, u32[]{:S(2)}) collective-permute-start(s32[2,512]{1,0:T(2,128)S(1)} %pad_add_fusion.2), channel_id=1, source_target_pairs={{0,3},{1,2},{2,5},{3,4},{4,7},{5,6},{6,9},{7,8},{8,11},{9,10},{10,... | collective-permute-start | bytes 12296 | tf_op jit(solution)/shard_map/ppermute | solution.py:594
  8.5 0.1 collective-permute-start.2
  8.6 1.4 fusion.7
  10.0 0.0 copy-start.5
  10.0 0.0 copy-start.6
  10.0 2.2 %fusion.2.own_ref = bf16[512,768]{1,0:T(8,128)(2,1)} fusion(bf16[512,768]{1,0:T(8,128)(2,1)} %param.5, f32[512]{0:T(512)S(1)} %add_rsqrt_fusion), kind=kLoop, calls=%fused_computation.4 | loop fusion | flops 1179648 | bytes 1574912 | tf_op jit(solution)/shard_map/convert_element_type | solution.py:603
  12.2 0.0 copy-done.4
  12.2 0.1 reshape.47
  12.3 0.1 copy.11
  12.5 0.9 reshape.48.wl_ref
  13.3 0.0 collective-permute-done.2
  13.4 0.0 copy-done.5
  13.4 0.0 copy-done.6
  13.4 1.0 copy.13.segq_ref
  14.4 0.0 collective-permute-done
  14.4 0.0 collective-permute-done.1
  14.5 0.6 and_select_fusion
  15.1 3.7 %fusion.8 = (f32[2048,32]{1,0:T(8,128)S(1)}, f32[2048,32]{1,0:T(8,128)S(1)}, f32[2048,32]{1,0:T(8,128)S(1)}) fusion(f32[32]{0:T(128)S(1)} %multiply_exponential_fusion, f32[2048]{0:T(1024)S(1)} %bitcast.7), kind=kLoop, calls=%fused_computation.14 | loop fusion | flops 131072 | bytes 794752 | tf_op jit(solution)/shard_map/neg | solution.py:550
  18.8 3.0 %pad_maximum_fusion = (f32[2048,128]{1,0:T(8,128)}, f32[2048,128]{1,0:T(8,128)}) fusion(f32[2048,32]{1,0:T(8,128)S(1)} %get-tuple-element.13, f32[2048,32]{1,0:T(8,128)S(1)} %get-tuple-element.12, f32[2048,32]{1,0:T(8,128)S(1)} %get-tuple-element.11), kind=kLoop, calls=%fused_computation.12 | loop fusion | flops 1572864 | bytes 2883584 | tf_op jit(solution)/shard_map/concatenate | solution.py:549
  21.8 0.0 copy-start
  21.8 132.8 %fused_attention.1 = (bf16[512,768]{1,0:T(8,128)(2,1)}, f32[512,768]{1,0:T(8,128)}, f32[48,2304]{1,0:T(8,128)}) custom-call(bf16[512,768]{1,0:T(8,128)(2,1)} %fusion.2.own_ref, bf16[2,3,48,384]{3,2,1,0:T(8,128)(2,1)} %reshape.48.wl_ref, f32[2048,128]{1,0:T(8,128)} %get-tuple-element.18.cos_ref, f32[2048,128]{1,0:T(8,128)} %get-tuple-element.19.sin_ref, ...), custom_call_target="tpu_custom_call" | custom-call | tf_op jit(solution)/shard_map/fused_attention/pallas_call | solution.py:489
  154.6 0.0 copy-start.1
  154.7 0.0 copy-done
  154.7 1.9 %fusion.3 = f32[512]{0:T(512)S(1)} fusion(f32[512,768]{1,0:T(8,128)} %get-tuple-element.7, bf16[512,768]{1,0:T(8,128)(2,1)S(1)} %copy-done, f32[512]{0:T(512)S(1)} %add_rsqrt_fusion), kind=kLoop, calls=%fused_computation.5 | loop fusion | flops 1572352 | bytes 2363392 | tf_op jit(solution)/shard_map/reduce_sum | solution.py:607
  156.6 0.0 copy-done.1
  156.6 0.0 copy-start.2
  156.6 1.2 fusion.6
  157.8 0.0 copy-start.3
  157.8 0.0 copy-done.2
  157.8 0.9 copy.16
  158.7 0.4 copy-done.3
  159.1 0.8 copy.17
  (7 shorter events, 0.1 us)
Async XLA Ops:
  0.6 11.6 %copy-start.4 = (bf16[48,2304]{1,0:T(8,128)(2,1)S(1)}, bf16[48,2304]{1,0:T(8,128)(2,1)}, u32[]{:S(2)}) copy-start(bf16[48,2304]{1,0:T(8,128)(2,1)} %param.6) | copy-start | bytes 663556
  1.4 13.0 %collective-permute-start = (s32[2,512]{1,0:T(2,128)S(1)}, s32[2,512]{1,0:T(2,128)S(1)}, u32[]{:S(2)}, u32[]{:S(2)}) collective-permute-start(s32[2,512]{1,0:T(2,128)S(1)} %pad_add_fusion.2), channel_id=1, source_target_pairs={{0,2},{1,3},{2,4},{3,5},{4,6},{5,7},{6,8},{7,9},{8,10},{9,11},{10,... | collective-permute-start | bytes 12296 | tf_op jit(solution)/shard_map/ppermute | solution.py:566
  4.6 9.9 %collective-permute-start.1 = (s32[2,512]{1,0:T(2,128)S(1)}, s32[2,512]{1,0:T(2,128)S(1)}, u32[]{:S(2)}, u32[]{:S(2)}) collective-permute-start(s32[2,512]{1,0:T(2,128)S(1)} %pad_add_fusion.2), channel_id=1, source_target_pairs={{0,3},{1,2},{2,5},{3,4},{4,7},{5,6},{6,9},{7,8},{8,11},{9,10},{10,... | collective-permute-start | bytes 12296 | tf_op jit(solution)/shard_map/ppermute | solution.py:594
  8.5 4.8 %collective-permute-start.2 = (s32[2,512]{1,0:T(2,128)S(1)}, s32[2,512]{1,0:T(2,128)S(1)}, u32[]{:S(2)}, u32[]{:S(2)}) collective-permute-start(s32[2,512]{1,0:T(2,128)S(1)} %pad_add_fusion.2), channel_id=1, source_target_pairs={{0,1},{1,0},{2,3},{3,2},{4,5},{5,4},{6,7},{7,6},{8,9},{9,8},{10,11... | collective-permute-start | bytes 12296 | tf_op jit(solution)/shard_map/ppermute | solution.py:560
  10.0 3.4 %copy-start.5 = (s32[512]{0:T(512)S(1)}, s32[512]{0:T(512)}, u32[]{:S(2)}) copy-start(s32[512]{0:T(512)} %param.8) | copy-start | bytes 6148
  10.0 3.4 %copy-start.6 = (s32[512]{0:T(512)S(1)}, s32[512]{0:T(512)}, u32[]{:S(2)}) copy-start(s32[512]{0:T(512)} %param.7) | copy-start | bytes 6148
  21.8 132.9 %copy-start = (bf16[512,768]{1,0:T(8,128)(2,1)S(1)}, bf16[512,768]{1,0:T(8,128)(2,1)}, u32[]{:S(2)}) copy-start(bf16[512,768]{1,0:T(8,128)(2,1)} %param.5) | copy-start | bytes 2359300
  154.6 1.9 %copy-start.1 = (f32[512,768]{1,0:T(8,128)S(1)}, f32[512,768]{1,0:T(8,128)}, u32[]{:S(2)}) copy-start(f32[512,768]{1,0:T(8,128)} %get-tuple-element.7) | copy-start | bytes 4718596
  156.6 1.2 copy-start.2
  157.8 1.3 copy-start.3
